TPU v7x, 256 devices: a whole 4x4x8 slice. The times are simulated.
256 devices in a mesh: layer: 16 (over z_lo, y), lat: 16 (over z_hi, x, core).
Axes of the slice: x: 4, y: 4, z: 8 (z_hi: 2, z_lo: 4; z = z_hi * 4 + z_lo), core: 2. Of those that a mesh axis runs over, the one named last changes fastest.
Arguments:
- inputs: bfloat16 [128, 4, 2048], P(None, None, 'layer'), may hold values from -6 to 6
- encoder: bfloat16 [4, 2048, 16384], P(None, 'layer', 'lat'), may hold values from -0.125 to 0.125
- enc_bias: float32 [4, 16384], P(None, 'lat'), may hold values from -3 to 3
- decoder: bfloat16 [16, 5, 16384, 256], P('layer', None, 'lat'), may hold values from -0.375 to 0.375
- dec_bias: float32 [16, 2, 256], P('layer'), may hold values from -3 to 3
- targets: bfloat16 [16, 128, 2, 256], P('layer'), may hold values from -6 to 6
- top_index: int32 [128, 4, 64], replicated, may hold values from 0 to 16383, as said below
Outputs:
- decoder_grad: float32 [16, 5, 16384, 256], P('layer', None, 'lat')
- encoder_grad: float32 [4, 2048, 16384], P(None, 'layer', 'lat')
- bias_grad: float32 [4, 16384], P(None, 'lat')
Inputs may be any that keep to these rules, and one draw needn't show every extreme that they name: `top_index`: the 64 entries of one token and layer are distinct; at most 8 of them have the same value of n // 1024, and every value of n // 1024 is taken by exactly 8 entries of some token and layer.
All inputs are finite; a program needn't handle non-finite values.
Results may differ from a plain program's by a relative error of at most 0.0045.
Values may be sent and summed in bfloat16 or wider, within the bound.
A program may use at most 64 MiB of HBM per device.

v0:
```python
import jax
import jax.numpy as jnp
from jax import lax
from jax.sharding import PartitionSpec as P

FEAT_SPLIT = 8


def pick_rows(weight_table, row_index):
    return jnp.take(weight_table, row_index, axis=0)


def body(inputs, encoder, enc_bias, decoder, dec_bias, targets, top_index):
    tokens, layers, top_count = top_index.shape
    slab_width = encoder.shape[2]
    slab_most = 2 * top_count // lax.axis_size("lat")
    pair_index = lax.axis_index("layer") // FEAT_SPLIT
    slab_index = lax.axis_index("lat")
    blocks = decoder.shape[1]
    decoder_own = decoder[0]
    local_index = top_index - slab_index * slab_width
    inside = (local_index >= 0) & (local_index < slab_width)
    position_ids = lax.broadcasted_iota(jnp.int32, top_index.shape, 2)
    order_key = jnp.where(inside, 2 * top_count, top_count) - position_ids
    slot_key, position = lax.top_k(order_key, slab_most)
    valid_slot = slot_key > top_count
    picked = jnp.take_along_axis(jnp.where(inside, local_index, 0), position, axis=2)
    encoder_rows = jnp.swapaxes(encoder, 1, 2)
    columns = jax.vmap(pick_rows, in_axes=(0, 1), out_axes=1)(encoder_rows, picked)
    partial_value = jnp.einsum("tld,tlsd->tls", inputs, columns, preferred_element_type=jnp.float32)
    pre_total = lax.psum(partial_value, "layer")
    bias_picked = jax.vmap(pick_rows, in_axes=(0, 1), out_axes=1)(enc_bias, picked)
    pre_value = (pre_total + bias_picked).astype(jnp.bfloat16)
    act_slots = lax.optimization_barrier(
        jnp.where(valid_slot, pre_value, jnp.zeros_like(pre_value))
    )
    token_ids = lax.broadcasted_iota(jnp.int32, picked.shape, 0)
    layer_ids = lax.broadcasted_iota(jnp.int32, picked.shape, 1)
    act_dense = (
        jnp.zeros((tokens, layers, slab_width), jnp.bfloat16)
        .at[token_ids, layer_ids, picked]
        .add(act_slots)
    )
    block_ids = jnp.arange(blocks, dtype=jnp.int32)
    first_target = block_ids <= pair_index
    source = jnp.where(first_target, block_ids, block_ids - pair_index - 1)
    slot_ids = jnp.where(first_target, 0, 1).astype(jnp.int32)
    slot_weight = jnp.stack([first_target, jnp.logical_not(first_target)], axis=1).astype(
        jnp.float32
    )
    source_onehot = (source[:, None] == jnp.arange(layers, dtype=jnp.int32)[None, :]).astype(
        jnp.float32
    )
    act_source = jnp.take(act_dense, source, axis=1)
    picked_source = jnp.take(picked, source, axis=1)
    per_block = jnp.einsum(
        "tks,ksf->tkf", act_source, decoder_own, preferred_element_type=jnp.float32
    )
    rebuilt = lax.psum(
        jnp.einsum("tkf,kc->tcf", per_block, slot_weight, precision=lax.Precision.HIGHEST), "lat"
    )
    residue = (rebuilt + dec_bias[0][None, :, :] - targets[0].astype(jnp.float32)).astype(
        jnp.bfloat16
    )
    residue = lax.optimization_barrier(residue)
    residue_block = jnp.take(residue, slot_ids, axis=1)
    block_grad = jnp.einsum(
        "tks,tkf->ksf", act_source, residue_block, preferred_element_type=jnp.float32
    )
    dense_grad = jnp.einsum(
        "tkf,ksf->tks", residue_block, decoder_own, preferred_element_type=jnp.float32
    )
    per_block = jnp.take_along_axis(dense_grad, picked_source, axis=2)
    grad_slots = lax.psum(
        jnp.einsum("tks,kl->tls", per_block, source_onehot, precision=lax.Precision.HIGHEST),
        "layer",
    ).astype(jnp.bfloat16)
    pre_grad = lax.optimization_barrier(
        jnp.where(valid_slot, grad_slots, jnp.zeros_like(grad_slots))
    )
    grad_dense = (
        jnp.zeros((tokens, layers, slab_width), jnp.bfloat16)
        .at[token_ids, layer_ids, picked]
        .add(pre_grad)
    )
    encoder_grad = jnp.einsum(
        "tld,tln->ldn", inputs, grad_dense, preferred_element_type=jnp.float32
    )
    bias_grad = jnp.sum(grad_dense, axis=0, dtype=jnp.float32)
    return (block_grad[None], encoder_grad, bias_grad)


def solution(mesh):
    return jax.shard_map(
        body,
        mesh=mesh,
        in_specs=(
            P(None, None, "layer"),
            P(None, "layer", "lat"),
            P(None, "lat"),
            P("layer", None, "lat", None),
            P("layer", None, None),
            P("layer", None, None, None),
            P(),
        ),
        out_specs=(P("layer", None, "lat", None), P(None, "layer", "lat"), P(None, "lat")),
        check_vma=False,
    )
```

profile of v0, /device:TPU:6, one launch (start us, length us, event | category | flops | bytes accessed | tf_op | source)
XLA Modules:
  0.0 725.0 jit_solution(8316755115968587439)
XLA Ops:
  9.3 1.7 top_k.12
  11.5 33.2 %gather_fusion.3 = s32[4096]{0:T(1024)S(1)} fusion(s32[128,4,64]{0,2,1:T(8,128)S(1)} %get-tuple-element.26, s32[4096]{0:T(1024)S(1)} %reshape.136), kind=kCustom, calls=%fused_computation.3 | custom fusion | bytes 81920 | tf_op jit(solution)/shard_map/jit(take_along_axis)/gather | solution.py:27
  46.1 34.9 %gather_fusion.5 = f32[4096]{0:T(1024)S(1)} fusion(f32[4,1024]{1,0:T(4,128)S(1)} %copy-done.1, s32[4096]{0:T(1024)S(1)} %reshape.142), kind=kCustom, calls=%fused_computation.5 | custom fusion | bytes 65536 | tf_op jit(solution)/shard_map/vmap(jit(_take))/gather | solution.py:10
  81.7 2.3 copy.62
  84.0 121.0 %gather_fusion.4 = bf16[4096,128]{1,0:T(8,128)(2,1)} fusion(bf16[4,1024,128]{2,1,0:T(8,128)(2,1)} %bitcast.88, s32[4096]{0:T(1024)S(1)} %reshape.142), kind=kCustom, calls=%fused_computation.4 | custom fusion | bytes 2129920 | tf_op jit(solution)/shard_map/vmap(jit(_take))/gather | solution.py:10
  205.0 2.1 fusion.16
  207.3 81.2 %psum.21 = f32[128,4,8]{0,1,2:T(4,128)S(1)} all-reduce(f32[128,4,8]{0,1,2:T(4,128)S(1)} %bitcast.91), channel_id=1, replica_groups=mesh['layer'=16,'lat'=16] {'layer'}, use_global_device_ids=true, to_apply=%region_1.2 | all-reduce | flops 4096 | bytes 32768 | tf_op jit(solution)/shard_map/psum | solution.py:31
  289.4 29.7 %scatter_custom_fusion = bf16[524288]{0:T(1024)(128)(2,1)} fusion(s32[4096]{0:T(1024)S(1)} %reshape.160, bf16[4096]{0:T(1024)(128)(2,1)S(1)} %reshape.162, bf16[]{:T(256)} %constant.131.clone.1), kind=kCustom, calls=%fused_computation.30 | custom fusion | flops 4096 | bytes 1048578
  319.1 2.1 reshape.106
  321.3 2.5 copy.66
  323.8 3.0 gather_fusion
  326.8 1.9 fusion.9
  328.8 1.7 convolution_bitcast_fusion.2
  332.6 170.9 %all-reduce.2.cloned.1.call-done = f32[128,2,256]{2,1,0:T(2,128)} async-done(((f32[128,2,256]{2,1,0:T(2,128)}), f32[128,2,256]{2,1,0:T(2,128)}) %all-reduce.2.cloned.1.call-update) | async-done | bytes 262160 | tf_op jit(solution)/shard_map/psum | solution.py:59
  503.5 1.1 fusion.24
  505.9 2.5 fusion.4
  508.4 85.5 %gather_fusion.6 = f32[5120]{0:T(1024)S(1)} fusion(f32[128,5,1024]{2,0,1:T(8,128)} %fusion.4, s32[5120]{0:T(1024)S(1)} %reshape.154), kind=kCustom, calls=%fused_computation.6 | custom fusion | bytes 102400 | tf_op jit(solution)/shard_map/jit(take_along_axis)/gather | solution.py:73
  594.5 79.3 %psum.23 = bf16[128,4,8]{0,1,2:T(4,128)(2,1)S(1)} all-reduce(f32[128,4,8]{0,1,2:T(4,128)S(1)} %convolution_bitcast_fusion.3), channel_id=1, replica_groups=mesh['layer'=16,'lat'=16] {'layer'}, use_global_device_ids=true, to_apply=%region_4.5 | all-reduce | flops 4096 | bytes 24576 | tf_op jit(solution)/shard_map/psum | solution.py:74
  674.2 29.9 %scatter_custom_fusion.1 = bf16[524288]{0:T(1024)(128)(2,1)} fusion(s32[4096]{0:T(1024)} %copy-done.10, bf16[4096]{0:T(1024)(128)(2,1)S(1)} %reshape.168, bf16[]{:T(256)} %constant.131.clone.1), kind=kCustom, calls=%fused_computation.28 | custom fusion | flops 4096 | bytes 1049088
  704.1 2.2 reshape.110
  706.2 2.4 convert_reduce_fusion
  708.7 3.2 convolution_bitcast_fusion.1
  711.9 3.4 convolution_bitcast_fusion
  715.2 2.9 copy.77
  (96 shorter events, 9.8 us)
Async XLA Ops:
  7.2 319.6 %copy-start = (bf16[1,5,1024,256]{3,2,1,0:T(8,128)(2,1)S(1)}, bf16[1,5,1024,256]{3,2,1,0:T(8,128)(2,1)}, u32[]{:S(2)}) copy-start(bf16[1,5,1024,256]{3,2,1,0:T(8,128)(2,1)} %param.10) | copy-start | bytes 7864324
  7.2 496.3 %all-reduce.2.cloned.1.call-start = ((), (), s32[]{:S(2)}) async-start(), calls=%async_computation | async-start | bytes 524288 | tf_op jit(solution)/shard_map/psum | solution.py:59
  11.5 33.9 %copy-start.20 = (s32[3]{0:T(128)S(1)}, s32[3]{0:T(128)}, u32[]{:S(2)}) copy-start(s32[3]{0:T(128)} %constant.147) | copy-start | bytes 40
  11.5 34.0 %copy-start.19 = (s32[3]{0:T(128)S(1)}, s32[3]{0:T(128)}, u32[]{:S(2)}) copy-start(s32[3]{0:T(128)} %constant.144) | copy-start | bytes 40
  44.8 1.4 copy-start.1
  81.7 207.7 %copy-start.10 = (s32[4096]{0:T(1024)}, s32[4096]{0:T(1024)S(1)}, u32[]{:S(2)}) copy-start(s32[4096]{0:T(1024)S(1)} %reshape.160) | copy-start | bytes 49156
  84.0 121.0 %copy-start.7 = (bf16[128,4,128]{2,1,0:T(4,128)(2,1)S(1)}, bf16[128,4,128]{2,1,0:T(4,128)(2,1)}, u32[]{:S(2)}) copy-start(bf16[128,4,128]{2,1,0:T(4,128)(2,1)} %param.7) | copy-start | bytes 393220
  323.8 3.0 copy-start.12
  326.8 2.0 copy-start.17
  326.8 2.0 copy-start.18
  328.7 174.7 %copy-start.9 = (bf16[1,128,2,256]{3,2,1,0:T(2,128)(2,1)S(1)}, bf16[1,128,2,256]{3,2,1,0:T(2,128)(2,1)}, u32[]{:S(2)}) copy-start(bf16[1,128,2,256]{3,2,1,0:T(2,128)(2,1)} %param.12) | copy-start | bytes 393220
  328.8 174.7 %copy-start.14 = (f32[1,2,256]{2,1,0:T(2,128)S(1)}, f32[1,2,256]{2,1,0:T(2,128)}, u32[]{:S(2)}) copy-start(f32[1,2,256]{2,1,0:T(2,128)} %param.11) | copy-start | bytes 6148
  330.5 177.9 %copy-start.15 = (pred[5]{0:T(512)(128)(4,1)}, pred[5]{0:T(512)(128)(4,1)S(1)}, u32[]{:S(2)}) copy-start(pred[5]{0:T(512)(128)(4,1)S(1)} %fusion.40) | copy-start | bytes 19
  331.1 0.6 copy-start.2
  505.2 0.7 copy-start.5
  508.4 85.8 %copy-start.3 = (s32[5,128,8]{1,2,0:T(8,128)S(1)}, s32[5,128,8]{1,2,0:T(8,128)}, u32[]{:S(2)}) copy-start(s32[5,128,8]{1,2,0:T(8,128)} %copy-done.2) | copy-start | bytes 61444
  508.4 85.8 %copy-start.13 = (pred[5]{0:T(512)(128)(4,1)S(1)}, pred[5]{0:T(512)(128)(4,1)}, u32[]{:S(2)}) copy-start(pred[5]{0:T(512)(128)(4,1)} %compare_and_fusion.2) | copy-start | bytes 19
  508.4 85.9 %copy-start.21 = (s32[5]{0:T(128)S(1)}, s32[5]{0:T(128)}, u32[]{:S(2)}) copy-start(s32[5]{0:T(128)} %compare_select_fusion.7) | copy-start | bytes 64
  508.4 165.4 %copy-start.11 = (pred[128,4,8]{0,1,2:T(4,128)(4,1)S(1)}, pred[128,4,8]{0,1,2:T(4,128)(4,1)}, u32[]{:S(2)}) copy-start(pred[128,4,8]{0,1,2:T(4,128)(4,1)} %get-tuple-element.22) | copy-start | bytes 12292
  674.2 34.5 %copy-start.8 = (bf16[128,4,128]{2,1,0:T(4,128)(2,1)S(1)}, bf16[128,4,128]{2,1,0:T(4,128)(2,1)}, u32[]{:S(2)}) copy-start(bf16[128,4,128]{2,1,0:T(4,128)(2,1)} %param.7) | copy-start | bytes 393220
  706.2 5.7 copy-start.4
  706.2 5.7 copy-start.6
  706.2 5.7 copy-start.16
Sparse Core Ops, SparseCore 0:
  330.6 172.8 all-reduce.1
where the time goes:
time: 729 us; the launch traced here: 725 us
  local copies, waits for them, and re-layouts  296 us (41%)
  waiting for transfers between devices  171 us (23%)
  blocking collectives  161 us (22%)
  other arithmetic  68.5 us (9%)
  matrix products  14.9 us (2%)
  between operations  14.5 us (2%)
    psum x1, waiting for transfers between devices, body(): lax.psum(jnp.einsum('tkf,kc->tcf', per_block, slot_weight, precision=lax....  171 us
    gather x6, local copies, waits for them, and re-layouts, pick_rows(): return jnp.take(weight_table, row_index, axis=0)  156 us
    gather x5, local copies, waits for them, and re-layouts, body(): per_block = jnp.take_along_axis(dense_grad, picked_source, axis=2)  86.2 us
    psum x1, blocking collectives, body(): pre_total = lax.psum(partial_value, 'layer')  81.2 us
    psum x1, blocking collectives, body(): lax.psum(jnp.einsum('tks,kl->tls', per_block, source_onehot, precision=la...  79.3 us
    unnamed x5, other arithmetic  59.8 us
    gather x5, local copies, waits for them, and re-layouts, body(): jnp.take_along_axis(jnp.where(inside, local_index, 0), position, axis=2)  34 us
  transfers between devices with their start and end apart: 1, of which 1 were waited for; matrix products, arithmetic and copies ran while one was open for 0% of the time, Pallas kernels for 0%

commit v1 on v0

v1 whole, which is shorter than its diff:
```python
import jax
import jax.numpy as jnp
from jax import lax
from jax.experimental import pallas as pl
from jax.experimental.pallas import tpu as pltpu
from jax.sharding import PartitionSpec as P

MESH = pl.DeviceIdType.MESH
F32 = jnp.float32
BF16 = jnp.bfloat16
I32 = jnp.int32

TOKENS, LAYERS, TOPK, WIDTH, DIN, FEAT, BLOCKS, SLOTS = 128, 4, 64, 1024, 128, 256, 5, 8
WIRE = F32


def pick(values, lanes):
    return jnp.take_along_axis(values, lanes, axis=1, mode="promise_in_bounds")


def main_kernel(x_hbm, enc_hbm, bias_hbm, dec_hbm, dbias_hbm, tgt_hbm, idx_hbm,
                act_ref, res_ref, pg_ref, xt_ref,
                x_v, enc_v, bias_v, dec_v, dbias_v, tgt_v, idx_v, load_sem,
                xf, dense, inv, code_v, low_v, high_v, rec, goal,
                ybuf1, zbuf1, ybuf2, zbuf2, rs_src, rs_buf, hbuf, abuf, val_v,
                y1_s, y1_r, z1_s, z1_r, y2_s, y2_r, z2_s, z2_r,
                rs_s, rs_r, h_s, h_r, ag_s, ag_r):
    r = lax.axis_index("layer")
    j = lax.axis_index("lat")
    y = lax.rem(r, 4)
    zl = lax.div(r, 4)
    q = lax.rem(j, 8)
    zh = lax.div(j, 8)
    g = lax.div(r, 8)

    loads = [
        pltpu.make_async_copy(idx_hbm, idx_v, load_sem.at[0]),
        pltpu.make_async_copy(x_hbm, x_v, load_sem.at[1]),
        pltpu.make_async_copy(enc_hbm, enc_v, load_sem.at[2]),
        pltpu.make_async_copy(bias_hbm, bias_v, load_sem.at[3]),
        pltpu.make_async_copy(dec_hbm, dec_v, load_sem.at[4]),
        pltpu.make_async_copy(dbias_hbm, dbias_v, load_sem.at[5]),
        pltpu.make_async_copy(tgt_hbm.at[pl.ds(q * 16, 16)], tgt_v, load_sem.at[6]),
    ]
    for copy in loads:
        copy.start()

    def ypeer(i):
        return {"layer": zl * 4 + lax.rem(y + i, 4)}

    def zpeer(i):
        return {"layer": lax.rem(zl + i, 4) * 4 + y}

    def qpeer(i):
        return {"lat": zh * 8 + lax.rem(q + i, 8)}

    hpeer = {"lat": (1 - zh) * 8 + q}

    barrier = pltpu.get_barrier_semaphore()
    for i in range(1, 4):
        pl.semaphore_signal(barrier, inc=1, device_id=ypeer(i), device_id_type=MESH)
        pl.semaphore_signal(barrier, inc=1, device_id=zpeer(i), device_id_type=MESH)
    for i in range(1, 8):
        pl.semaphore_signal(barrier, inc=1, device_id=qpeer(i), device_id_type=MESH)
    pl.semaphore_signal(barrier, inc=1, device_id=hpeer, device_id_type=MESH)

    lane = lax.broadcasted_iota(I32, (32, 128), 1)
    quarter = lax.shift_right_logical(lane, 5)

    loads[0].wait()
    tri = (lax.broadcasted_iota(I32, (TOPK, TOPK), 1)
           < lax.broadcasted_iota(I32, (TOPK, TOPK), 0)).astype(F32).astype(BF16)
    sub8 = lax.broadcasted_iota(I32, (SLOTS, 128), 0)
    packs = []
    for l in range(LAYERS):
        local = idx_v[l] - j * WIDTH
        inside = (local >= 0) & (local < WIDTH)
        rank = jnp.dot(tri, inside.astype(F32).astype(BF16), preferred_element_type=F32)
        rank = jnp.where(inside, rank, -1.0)
        value = (local + (l * WIDTH + 1)).astype(F32)
        slot_rows = jnp.zeros((SLOTS, 128), F32)
        for s in range(SLOTS):
            row = jnp.sum(jnp.where(rank == float(s), value, 0.0), axis=0, keepdims=True)
            slot_rows = jnp.where(sub8 == s, row, slot_rows)
        packs.append(slot_rows)
    packed = jnp.concatenate(packs * 4, axis=0)
    code = jnp.transpose(packed).astype(I32) - 1
    code_v[...] = code
    low_v[...] = code & 127
    high_v[...] = lax.shift_right_arithmetic(code, 7)

    loads[1].wait()
    loads[2].wait()
    loads[3].wait()
    xf[...] = x_v[...].astype(F32)
    own = jnp.where(r == 0, 1.0, 0.0)
    for l in range(LAYERS):
        x_l = xf[pl.ds(l, TOKENS, stride=4), :]
        dense[l] = (jnp.dot(x_l.astype(BF16), enc_v[l], preferred_element_type=F32)
                    + bias_v[pl.ds(l, 1), :] * own)

    def gather():
        def step(tq, out):
            rows = pl.ds(pl.multiple_of(tq * 32, 32), 32)
            low = low_v[rows, :]
            high = high_v[rows, :]
            got = jnp.zeros((32, 128), F32)
            for b in range(32):
                block = dense[b // 8, rows, pl.ds((b % 8) * 128, 128)]
                got = jnp.where(high == b, pick(block, low), got)
            return jnp.where(quarter == tq, got, out)

        return lax.fori_loop(0, 4, step, jnp.zeros((32, 128), F32))

    def scatter(out_ref):
        def step(tq, carry):
            rows = pl.ds(pl.multiple_of(tq * 32, 32), 32)
            values = val_v[...]
            for b in range(32):
                cols = pl.ds((b % 8) * 128, 128)
                where = inv[b // 8, rows, cols]
                got = jnp.where(where >= 0, pick(values, where & 127), 0.0)
                out_ref[b // 8, rows, cols] = got.astype(BF16)
            return carry

        lax.fori_loop(0, 4, step, 0)

    def send(src, dst, s_sem, r_sem, peer):
        copy = pltpu.make_async_remote_copy(
            src_ref=src, dst_ref=dst, send_sem=s_sem, recv_sem=r_sem,
            device_id=peer, device_id_type=MESH)
        copy.start()
        return copy

    def exchange(buf, me, n, peer, s_sem, r_sem, between=None):
        sends = [send(buf.at[me], buf.at[me], s_sem.at[i], r_sem.at[me], peer(i))
                 for i in range(n - 1, 0, -1)]
        if between is not None:
            between()
        for i in range(1, n):
            other = lax.rem(me + i, n)
            pltpu.make_async_remote_copy(
                src_ref=buf.at[other], dst_ref=buf.at[other], send_sem=s_sem.at[i],
                recv_sem=r_sem.at[other], device_id=peer(i), device_id_type=MESH).wait_recv()
        for copy in sends:
            copy.wait_send()

    def total(buf, n):
        acc = buf[0].astype(F32)
        for i in range(1, n):
            acc = acc + buf[i].astype(F32)
        return acc

    def build_inverse():
        def step(c, carry):
            rows = pl.ds(pl.multiple_of(c * 16, 16), 16)
            base = lax.div(c, 2) * 32
            lane16 = lax.broadcasted_iota(I32, (16, 128), 1)
            code_rows = code_v[rows, :]
            for l in range(LAYERS):
                found = [jnp.full((16, 128), -1, I32) for h in range(8)]
                for s in range(SLOTS):
                    col = l * SLOTS + s
                    at = jnp.broadcast_to(code_rows[:, col:col + 1], (16, 128)) - l * WIDTH
                    for h in range(8):
                        found[h] = jnp.where(at == lane16 + h * 128, base + col, found[h])
                for h in range(8):
                    inv[l, rows, pl.ds(h * 128, 128)] = found[h]
            return carry

        lax.fori_loop(0, 8, step, 0)
        loads[5].wait()
        loads[6].wait()
        goal_all = tgt_v[...].astype(F32)
        for c in range(2):
            goal[c] = goal_all[:, c, :]

    def transpose_inputs():
        for l in range(LAYERS):
            xt_ref[l] = jnp.transpose(xf[pl.ds(l, TOKENS, stride=4), :]).astype(BF16)

    ybuf1[y] = gather().astype(WIRE)
    pl.semaphore_wait(barrier, 14)
    exchange(ybuf1, y, 4, ypeer, y1_s, y1_r, between=build_inverse)
    zbuf1[zl] = total(ybuf1, 4).astype(WIRE)
    exchange(zbuf1, zl, 4, zpeer, z1_s, z1_r, between=transpose_inputs)
    val_v[...] = total(zbuf1, 4).astype(BF16).astype(F32)
    scatter(act_ref)

    loads[4].wait()
    first = jnp.where(g == 1, 0, 1)

    def source_of(k):
        return jnp.where(k <= g, k, k - g - 1)

    def slot_of(k):
        return jnp.where(k <= g, 0, 1)

    def rebuild(k):
        return jnp.dot(act_ref[source_of(k)], dec_v[k], preferred_element_type=F32)

    rec[0] = rebuild(0)
    rec[1] = rebuild(2) + rebuild(3) + rebuild(4)
    rec[first] = rec[first] + rebuild(1)
    for c in range(2):
        rs_src[:, c] = rec[c].reshape(8, 16, FEAT).astype(BF16)
    rs_buf[q] = rs_src[q]
    sends = []
    for i in (4, 3, 5, 2, 6, 1, 7):
        other = lax.rem(q + i, 8)
        sends.append(send(rs_src.at[other], rs_buf.at[q], rs_s.at[i], rs_r.at[q], qpeer(i)))
    dense[...] = jnp.zeros_like(dense)
    for i in range(1, 8):
        other = lax.rem(q + i, 8)
        pltpu.make_async_remote_copy(
            src_ref=rs_buf.at[other], dst_ref=rs_buf.at[other], send_sem=rs_s.at[i],
            recv_sem=rs_r.at[other], device_id=qpeer(i), device_id_type=MESH).wait_recv()
    for copy in sends:
        copy.wait_send()
    hbuf[zh] = total(rs_buf, 8).astype(hbuf.dtype)
    copy = send(hbuf.at[zh], hbuf.at[zh], h_s, h_r.at[zh], hpeer)
    pltpu.make_async_remote_copy(
        src_ref=hbuf.at[1 - zh], dst_ref=hbuf.at[1 - zh], send_sem=h_s,
        recv_sem=h_r.at[1 - zh], device_id=hpeer, device_id_type=MESH).wait_recv()
    copy.wait_send()
    rebuilt = total(hbuf, 2)
    for c in range(2):
        abuf[q, c] = (rebuilt[c] + dbias_v[pl.ds(c, 1), :] - goal[c]).astype(BF16)
    exchange(abuf, q, 8, qpeer, ag_s, ag_r)

    for k in range(BLOCKS):
        residue = abuf[:, slot_of(k)].reshape(TOKENS, FEAT)
        dense[source_of(k)] = dense[source_of(k)] + lax.dot_general(
            residue, dec_v[k], (((1,), (1,)), ((), ())), preferred_element_type=F32)
    ybuf2[y] = gather().astype(WIRE)
    def keep_residue():
        res_ref[...] = abuf[...]

    exchange(ybuf2, y, 4, ypeer, y2_s, y2_r, between=keep_residue)
    zbuf2[zl] = total(ybuf2, 4).astype(WIRE)
    exchange(zbuf2, zl, 4, zpeer, z2_s, z2_r)
    val_v[...] = total(zbuf2, 4).astype(BF16).astype(F32)
    scatter(pg_ref)


def main_call(x, enc, bias, dec, dbias, tgt, idx):
    dma = pltpu.SemaphoreType.DMA
    vmem = pltpu.VMEM
    return pl.pallas_call(
        main_kernel,
        out_shape=(
            jax.ShapeDtypeStruct((LAYERS, TOKENS, WIDTH), BF16),
            jax.ShapeDtypeStruct((8, 2, 16, FEAT), BF16),
            jax.ShapeDtypeStruct((LAYERS, TOKENS, WIDTH), BF16),
            jax.ShapeDtypeStruct((LAYERS, DIN, TOKENS), BF16),
        ),
        in_specs=[pl.BlockSpec(memory_space=pl.ANY)] * 7,
        out_specs=(pl.BlockSpec(memory_space=pltpu.VMEM),) * 4,
        scratch_shapes=[
            vmem((TOKENS * LAYERS, DIN), BF16),
            vmem((LAYERS, DIN, WIDTH), BF16),
            vmem((LAYERS, WIDTH), F32),
            vmem((BLOCKS, WIDTH, FEAT), BF16),
            vmem((2, FEAT), F32),
            vmem((16, 2, FEAT), BF16),
            vmem((LAYERS, TOPK, TOKENS), I32),
            dma((7,)),
            vmem((TOKENS * LAYERS, DIN), F32),
            vmem((LAYERS, TOKENS, WIDTH), F32),
            vmem((LAYERS, TOKENS, WIDTH), I32),
            vmem((TOKENS, 128), I32),
            vmem((TOKENS, 128), I32),
            vmem((TOKENS, 128), I32),
            vmem((2, TOKENS, FEAT), F32),
            vmem((2, 16, FEAT), F32),
            vmem((4, 32, 128), WIRE),
            vmem((4, 32, 128), WIRE),
            vmem((4, 32, 128), WIRE),
            vmem((4, 32, 128), WIRE),
            vmem((8, 2, 16, FEAT), BF16),
            vmem((8, 2, 16, FEAT), BF16),
            vmem((2, 2, 16, FEAT), WIRE),
            vmem((8, 2, 16, FEAT), BF16),
            vmem((32, 128), F32),
            dma((4,)), dma((4,)), dma((4,)), dma((4,)),
            dma((4,)), dma((4,)), dma((4,)), dma((4,)),
            dma((8,)), dma((8,)), dma, dma((2,)), dma((8,)), dma((8,)),
        ],
        compiler_params=pltpu.CompilerParams(collective_id=0, has_side_effects=True),
        name="transcoder",
    )(x, enc, bias, dec, dbias, tgt, idx)


def grad_kernel(act_ref, res_ref, pg_ref, xt_ref, dg_ref, eg_ref, bg_ref):
    k = pl.program_id(0)
    g = lax.div(lax.axis_index("layer"), 8)
    source = jnp.where(k <= g, k, k - g - 1)
    slot = jnp.where(k <= g, 0, 1)
    residue = res_ref[:, slot].reshape(TOKENS, FEAT)
    dg_ref[0] = lax.dot_general(act_ref[source], residue, (((0,), (0,)), ((), ())),
                                preferred_element_type=F32)

    @pl.when(k < LAYERS)
    def _():
        grads = pg_ref[k]
        eg_ref[0] = jnp.dot(xt_ref[k], grads, preferred_element_type=F32)
        bg_ref[pl.ds(k, 1), :] = jnp.dot(jnp.ones((8, TOKENS), BF16), grads,
                                         preferred_element_type=F32)[0:1]


def grad_call(act, res, pg, xt):
    def whole(*shape):
        return pl.BlockSpec(shape, lambda k: (0,) * len(shape))

    return pl.pallas_call(
        grad_kernel,
        grid=(BLOCKS,),
        out_shape=(
            jax.ShapeDtypeStruct((BLOCKS, WIDTH, FEAT), F32),
            jax.ShapeDtypeStruct((LAYERS, DIN, WIDTH), F32),
            jax.ShapeDtypeStruct((LAYERS, WIDTH), F32),
        ),
        in_specs=[whole(LAYERS, TOKENS, WIDTH), whole(8, 2, 16, FEAT),
                  whole(LAYERS, TOKENS, WIDTH), whole(LAYERS, DIN, TOKENS)],
        out_specs=(
            pl.BlockSpec((1, WIDTH, FEAT), lambda k: (k, 0, 0)),
            pl.BlockSpec((1, DIN, WIDTH), lambda k: (jnp.minimum(k, LAYERS - 1), 0, 0)),
            whole(LAYERS, WIDTH),
        ),
        name="weight_grads",
    )(act, res, pg, xt)


def body(inputs, encoder, enc_bias, decoder, dec_bias, targets, top_index):
    act, res, pg, xt = main_call(
        inputs.reshape(TOKENS * LAYERS, DIN), encoder, enc_bias, decoder[0], dec_bias[0],
        targets[0], jnp.transpose(top_index, (1, 2, 0)))
    dg, eg, bg = grad_call(act, res, pg, xt)
    return dg[None], eg, bg


def solution(mesh):
    return jax.shard_map(
        body,
        mesh=mesh,
        in_specs=(
            P(None, None, "layer"),
            P(None, "layer", "lat"),
            P(None, "lat"),
            P("layer", None, "lat", None),
            P("layer", None, None),
            P("layer", None, None, None),
            P(),
        ),
        out_specs=(P("layer", None, "lat", None), P(None, "layer", "lat"), P(None, "lat")),
        check_vma=False,
    )
```

time: 729 us -> 51.9 us (0.07)
  the two profiles are of different devices: /device:TPU:6 before, /device:TPU:1 now
where the time goes in v1:
time: 51.9 us; the launch traced here: 51.3 us
  Pallas kernels  50.6 us (97%)
  between operations  0.64 us (1%)
    pallas_call x1, Pallas kernels, main_call(): pl.pallas_call(main_kernel, out_shape=(jax.ShapeDtypeStruct((LAYERS, TOKE...  44.1 us
    pallas_call x1, Pallas kernels, grad_call(): pl.pallas_call(grad_kernel, grid=(BLOCKS,), out_shape=(jax.ShapeDtypeStru...  6.53 us

profile of v1, /device:TPU:1, one launch (start us, length us, event | category | flops | bytes accessed | tf_op | source)
XLA Modules:
  0.0 51.3 jit_solution(6604098183441602857)
XLA Ops:
  0.6 44.1 %transcoder.1 = (bf16[4,128,1024]{2,1,0:T(8,128)(2,1)}, bf16[8,2,16,256]{3,2,1,0:T(8,128)(2,1)}, bf16[4,128,1024]{2,1,0:T(8,128)(2,1)}, bf16[4,128,128]{2,1,0:T(8,128)(2,1)}) custom-call(bf16[512,128]{1,0:T(8,128)(2,1)} %bitcast.7, bf16[4,128,1024]{2,1,0:T(8,128)(2,1)} %enc_hbm.1, f32[4,1024]{1,0:T(4,128)} %bias_hbm.1, bf16[5,1024,256]{2,1,0:T(8,128)(2,1)} %bitcast.6, ...), custom_call_target="tpu_custom_call" | custom-call | tf_op jit(solution)/shard_map/transcoder/pallas_call | solution.py:249
  44.7 6.5 %weight_grads.1 = (f32[5,1024,256]{2,1,0:T(8,128)}, f32[4,128,1024]{2,1,0:T(8,128)}, f32[4,1024]{1,0:T(4,128)}) custom-call(bf16[4,128,1024]{2,1,0:T(8,128)(2,1)} %get-tuple-element.10.act_ref, bf16[8,2,16,256]{3,2,1,0:T(8,128)(2,1)} %get-tuple-element.11.res_ref, bf16[4,128,1024]{2,1,0:T(8,128)(2,1)} %get-tuple-element.12.pg_ref, ...), custom_call_target="tpu_custom_call" | custom-call | tf_op jit(solution)/shard_map/weight_grads/pallas_call | solution.py:315

commit v2 on v1

--- a/solution.py
+++ b/solution.py
@@ -42,8 +42,8 @@
         pltpu.make_async_copy(dbias_hbm, dbias_v, load_sem.at[5]),
         pltpu.make_async_copy(tgt_hbm.at[pl.ds(q * 16, 16)], tgt_v, load_sem.at[6]),
     ]
-    for copy in loads:
-        copy.start()
+    for n in (0, 1, 2, 3, 5, 6):
+        loads[n].start()
 
     def ypeer(i):
         return {"layer": zl * 4 + lax.rem(y + i, 4)}
@@ -93,6 +93,7 @@
     loads[2].wait()
     loads[3].wait()
     xf[...] = x_v[...].astype(F32)
+    loads[4].start()
     own = jnp.where(r == 0, 1.0, 0.0)
     for l in range(LAYERS):
         x_l = xf[pl.ds(l, TOKENS, stride=4), :]
@@ -254,7 +255,7 @@
             jax.ShapeDtypeStruct((LAYERS, TOKENS, WIDTH), BF16),
             jax.ShapeDtypeStruct((LAYERS, DIN, TOKENS), BF16),
         ),
-        in_specs=[pl.BlockSpec(memory_space=pl.ANY)] * 7,
+        in_specs=[pl.BlockSpec(memory_space=pltpu.HBM)] * 7,
         out_specs=(pl.BlockSpec(memory_space=pltpu.VMEM),) * 4,
         scratch_shapes=[
             vmem((TOKENS * LAYERS, DIN), BF16),
@@ -286,47 +287,49 @@
             dma((4,)), dma((4,)), dma((4,)), dma((4,)),
             dma((8,)), dma((8,)), dma, dma((2,)), dma((8,)), dma((8,)),
         ],
-        compiler_params=pltpu.CompilerParams(collective_id=0, has_side_effects=True),
+        compiler_params=pltpu.CompilerParams(collective_id=0, has_side_effects=True,
+                                             vmem_limit_bytes=24 * 2**20),
         name="transcoder",
-    )(x, enc, bias, dec, dbias, tgt, idx)
-
-
-def grad_kernel(act_ref, res_ref, pg_ref, xt_ref, dg_ref, eg_ref, bg_ref):
-    k = pl.program_id(0)
+    )(*[pltpu.with_memory_space_constraint(v, pltpu.HBM) for v in (x, enc, bias, dec, dbias, tgt, idx)])
+
+
+def grad_kernel(act_ref, res_ref, pg_ref, xt_ref, dg_hbm, eg_hbm, bg_ref, dg_v, eg_v, sem):
     g = lax.div(lax.axis_index("layer"), 8)
-    source = jnp.where(k <= g, k, k - g - 1)
-    slot = jnp.where(k <= g, 0, 1)
-    residue = res_ref[:, slot].reshape(TOKENS, FEAT)
-    dg_ref[0] = lax.dot_general(act_ref[source], residue, (((0,), (0,)), ((), ())),
-                                preferred_element_type=F32)
-
-    @pl.when(k < LAYERS)
-    def _():
-        grads = pg_ref[k]
-        eg_ref[0] = jnp.dot(xt_ref[k], grads, preferred_element_type=F32)
-        bg_ref[pl.ds(k, 1), :] = jnp.dot(jnp.ones((8, TOKENS), BF16), grads,
+    copies = []
+    for k in range(LAYERS):
+        eg_v[k] = jnp.dot(xt_ref[k], pg_ref[k], preferred_element_type=F32)
+        copies.append(pltpu.make_async_copy(eg_v.at[k], eg_hbm.at[k], sem.at[BLOCKS + k]))
+        copies[-1].start()
+    for k in range(BLOCKS):
+        source = jnp.where(k <= g, k, k - g - 1)
+        slot = jnp.where(k <= g, 0, 1)
+        residue = res_ref[:, slot].reshape(TOKENS, FEAT)
+        dg_v[k] = lax.dot_general(act_ref[source], residue, (((0,), (0,)), ((), ())),
+                                  preferred_element_type=F32)
+        copies.append(pltpu.make_async_copy(dg_v.at[k], dg_hbm.at[k], sem.at[k]))
+        copies[-1].start()
+    for k in range(LAYERS):
+        bg_ref[pl.ds(k, 1), :] = jnp.dot(jnp.ones((8, TOKENS), BF16), pg_ref[k],
                                          preferred_element_type=F32)[0:1]
+    for copy in copies:
+        copy.wait()
 
 
 def grad_call(act, res, pg, xt):
-    def whole(*shape):
-        return pl.BlockSpec(shape, lambda k: (0,) * len(shape))
-
+    vmem = pltpu.VMEM
     return pl.pallas_call(
         grad_kernel,
-        grid=(BLOCKS,),
         out_shape=(
             jax.ShapeDtypeStruct((BLOCKS, WIDTH, FEAT), F32),
             jax.ShapeDtypeStruct((LAYERS, DIN, WIDTH), F32),
             jax.ShapeDtypeStruct((LAYERS, WIDTH), F32),
         ),
-        in_specs=[whole(LAYERS, TOKENS, WIDTH), whole(8, 2, 16, FEAT),
-                  whole(LAYERS, TOKENS, WIDTH), whole(LAYERS, DIN, TOKENS)],
-        out_specs=(
-            pl.BlockSpec((1, WIDTH, FEAT), lambda k: (k, 0, 0)),
-            pl.BlockSpec((1, DIN, WIDTH), lambda k: (jnp.minimum(k, LAYERS - 1), 0, 0)),
-            whole(LAYERS, WIDTH),
-        ),
+        in_specs=[pl.BlockSpec(memory_space=vmem)] * 4,
+        out_specs=(pl.BlockSpec(memory_space=pl.ANY), pl.BlockSpec(memory_space=pl.ANY),
+                   pl.BlockSpec(memory_space=vmem)),
+        scratch_shapes=[vmem((BLOCKS, WIDTH, FEAT), F32), vmem((LAYERS, DIN, WIDTH), F32),
+                        pltpu.SemaphoreType.DMA((BLOCKS + LAYERS,))],
+        compiler_params=pltpu.CompilerParams(vmem_limit_bytes=24 * 2**20),
         name="weight_grads",
     )(act, res, pg, xt)
 

time: 51.9 us -> 48.1 us (0.927)
  Pallas kernels: 50.6 us -> 46.8 us
    pallas_call x1, Pallas kernels: 6.53 us -> 3.88 us  [grad_call(): pl.pallas_call(grad_kernel, out_shape=(jax.ShapeDtypeStruct((BLOCKS, WIDT...]
    pallas_call x1, Pallas kernels: 44.1 us -> 42.9 us  [main_call(): pl.pallas_call(main_kernel, out_shape=(jax.ShapeDtypeStruct((LAYERS, TOKE...]
where the time goes in v2:
time: 48.1 us; the launch traced here: 47.4 us
  Pallas kernels  46.8 us (97%)
  between operations  0.64 us (1%)
    pallas_call x1, Pallas kernels, main_call(): pl.pallas_call(main_kernel, out_shape=(jax.ShapeDtypeStruct((LAYERS, TOKE...  42.9 us
    pallas_call x1, Pallas kernels, grad_call(): pl.pallas_call(grad_kernel, out_shape=(jax.ShapeDtypeStruct((BLOCKS, WIDT...  3.88 us

profile of v2, /device:TPU:1, one launch (start us, length us, event | category | flops | bytes accessed | tf_op | source)
XLA Modules:
  0.0 47.4 jit_solution(18254304377482939252)
XLA Ops:
  0.6 42.9 %transcoder.1 = (bf16[4,128,1024]{2,1,0:T(8,128)(2,1)S(1)}, bf16[8,2,16,256]{3,2,1,0:T(8,128)(2,1)S(1)}, bf16[4,128,1024]{2,1,0:T(8,128)(2,1)S(1)}, bf16[4,128,128]{2,1,0:T(8,128)(2,1)S(1)}) custom-call(bf16[512,128]{1,0:T(8,128)(2,1)} %bitcast.7, bf16[4,128,1024]{2,1,0:T(8,128)(2,1)} %enc_hbm.1, f32[4,1024]{1,0:T(4,128)} %bias_hbm.1, ...), custom_call_target="tpu_custom_call" | custom-call | tf_op jit(solution)/shard_map/transcoder/pallas_call | solution.py:250
  43.6 3.9 %weight_grads.1 = (f32[5,1024,256]{2,1,0:T(8,128)}, f32[4,128,1024]{2,1,0:T(8,128)}, f32[4,1024]{1,0:T(4,128)}) custom-call(bf16[4,128,1024]{2,1,0:T(8,128)(2,1)S(1)} %get-tuple-element.10.act_ref, bf16[8,2,16,256]{3,2,1,0:T(8,128)(2,1)S(1)} %get-tuple-element.11.res_ref, bf16[4,128,1024]{2,1,0:T(8,128)(2,1)S(1)} %get-tuple-element.12.pg_ref, ...), custom_call_target="tpu_custom_call" | custom-call | tf_op jit(solution)/shard_map/weight_grads/pallas_call | solution.py:320

commit v3 on v2

--- a/solution.py
+++ b/solution.py
@@ -11,7 +11,7 @@
 I32 = jnp.int32
 
 TOKENS, LAYERS, TOPK, WIDTH, DIN, FEAT, BLOCKS, SLOTS = 128, 4, 64, 1024, 128, 256, 5, 8
-WIRE = F32
+WIRE = BF16
 
 
 def pick(values, lanes):
@@ -22,13 +22,11 @@
                 act_ref, res_ref, pg_ref, xt_ref,
                 x_v, enc_v, bias_v, dec_v, dbias_v, tgt_v, idx_v, load_sem,
                 xf, dense, inv, code_v, low_v, high_v, rec, goal,
-                ybuf1, zbuf1, ybuf2, zbuf2, rs_src, rs_buf, hbuf, abuf, val_v,
-                y1_s, y1_r, z1_s, z1_r, y2_s, y2_r, z2_s, z2_r,
+                lbuf1, lbuf2, rs_src, rs_buf, hbuf, abuf, val_v,
+                l1_s, l1_r, l2_s, l2_r,
                 rs_s, rs_r, h_s, h_r, ag_s, ag_r):
     r = lax.axis_index("layer")
     j = lax.axis_index("lat")
-    y = lax.rem(r, 4)
-    zl = lax.div(r, 4)
     q = lax.rem(j, 8)
     zh = lax.div(j, 8)
     g = lax.div(r, 8)
@@ -45,11 +43,8 @@
     for n in (0, 1, 2, 3, 5, 6):
         loads[n].start()
 
-    def ypeer(i):
-        return {"layer": zl * 4 + lax.rem(y + i, 4)}
-
-    def zpeer(i):
-        return {"layer": lax.rem(zl + i, 4) * 4 + y}
+    def lpeer(i):
+        return {"layer": lax.rem(r + i, 16)}
 
     def qpeer(i):
         return {"lat": zh * 8 + lax.rem(q + i, 8)}
@@ -57,9 +52,8 @@
     hpeer = {"lat": (1 - zh) * 8 + q}
 
     barrier = pltpu.get_barrier_semaphore()
-    for i in range(1, 4):
-        pl.semaphore_signal(barrier, inc=1, device_id=ypeer(i), device_id_type=MESH)
-        pl.semaphore_signal(barrier, inc=1, device_id=zpeer(i), device_id_type=MESH)
+    for i in range(1, 16):
+        pl.semaphore_signal(barrier, inc=1, device_id=lpeer(i), device_id_type=MESH)
     for i in range(1, 8):
         pl.semaphore_signal(barrier, inc=1, device_id=qpeer(i), device_id_type=MESH)
     pl.semaphore_signal(barrier, inc=1, device_id=hpeer, device_id_type=MESH)
@@ -180,12 +174,15 @@
         for l in range(LAYERS):
             xt_ref[l] = jnp.transpose(xf[pl.ds(l, TOKENS, stride=4), :]).astype(BF16)
 
-    ybuf1[y] = gather().astype(WIRE)
-    pl.semaphore_wait(barrier, 14)
-    exchange(ybuf1, y, 4, ypeer, y1_s, y1_r, between=build_inverse)
-    zbuf1[zl] = total(ybuf1, 4).astype(WIRE)
-    exchange(zbuf1, zl, 4, zpeer, z1_s, z1_r, between=transpose_inputs)
-    val_v[...] = total(zbuf1, 4).astype(BF16).astype(F32)
+    lbuf1[r] = gather().astype(WIRE)
+    pl.semaphore_wait(barrier, 23)
+
+    def hidden():
+        build_inverse()
+        transpose_inputs()
+
+    exchange(lbuf1, r, 16, lpeer, l1_s, l1_r, between=hidden)
+    val_v[...] = total(lbuf1, 16).astype(BF16).astype(F32)
     scatter(act_ref)
 
     loads[4].wait()
@@ -233,14 +230,13 @@
         residue = abuf[:, slot_of(k)].reshape(TOKENS, FEAT)
         dense[source_of(k)] = dense[source_of(k)] + lax.dot_general(
             residue, dec_v[k], (((1,), (1,)), ((), ())), preferred_element_type=F32)
-    ybuf2[y] = gather().astype(WIRE)
+    lbuf2[r] = gather().astype(WIRE)
+
     def keep_residue():
         res_ref[...] = abuf[...]
 
-    exchange(ybuf2, y, 4, ypeer, y2_s, y2_r, between=keep_residue)
-    zbuf2[zl] = total(ybuf2, 4).astype(WIRE)
-    exchange(zbuf2, zl, 4, zpeer, z2_s, z2_r)
-    val_v[...] = total(zbuf2, 4).astype(BF16).astype(F32)
+    exchange(lbuf2, r, 16, lpeer, l2_s, l2_r, between=keep_residue)
+    val_v[...] = total(lbuf2, 16).astype(BF16).astype(F32)
     scatter(pg_ref)
 
 
@@ -274,17 +270,14 @@
             vmem((TOKENS, 128), I32),
             vmem((2, TOKENS, FEAT), F32),
             vmem((2, 16, FEAT), F32),
-            vmem((4, 32, 128), WIRE),
-            vmem((4, 32, 128), WIRE),
-            vmem((4, 32, 128), WIRE),
-            vmem((4, 32, 128), WIRE),
+            vmem((16, 32, 128), WIRE),
+            vmem((16, 32, 128), WIRE),
             vmem((8, 2, 16, FEAT), BF16),
             vmem((8, 2, 16, FEAT), BF16),
             vmem((2, 2, 16, FEAT), WIRE),
             vmem((8, 2, 16, FEAT), BF16),
             vmem((32, 128), F32),
-            dma((4,)), dma((4,)), dma((4,)), dma((4,)),
-            dma((4,)), dma((4,)), dma((4,)), dma((4,)),
+            dma((16,)), dma((16,)), dma((16,)), dma((16,)),
             dma((8,)), dma((8,)), dma, dma((2,)), dma((8,)), dma((8,)),
         ],
         compiler_params=pltpu.CompilerParams(collective_id=0, has_side_effects=True,

time: 48.1 us -> 45.9 us (0.954); the launches traced: 47.4 us -> 45.8 us
  Pallas kernels: 46.8 us -> 45.2 us
    pallas_call x1, Pallas kernels: 42.9 us -> 41.3 us  [main_call(): pl.pallas_call(main_kernel, out_shape=(jax.ShapeDtypeStruct((LAYERS, TOKE...]
where the time goes in v3:
time: 45.9 us; the launch traced here: 45.8 us
  Pallas kernels  45.2 us (98%)
  between operations  0.64 us (1%)
    pallas_call x1, Pallas kernels, main_call(): pl.pallas_call(main_kernel, out_shape=(jax.ShapeDtypeStruct((LAYERS, TOKE...  41.3 us
    pallas_call x1, Pallas kernels, grad_call(): pl.pallas_call(grad_kernel, out_shape=(jax.ShapeDtypeStruct((BLOCKS, WIDT...  3.88 us

profile of v3, /device:TPU:1, one launch (start us, length us, event | category | flops | bytes accessed | tf_op | source)
XLA Modules:
  0.0 45.8 jit_solution(4088610414448896011)
XLA Ops:
  0.6 41.3 %transcoder.1 = (bf16[4,128,1024]{2,1,0:T(8,128)(2,1)S(1)}, bf16[8,2,16,256]{3,2,1,0:T(8,128)(2,1)S(1)}, bf16[4,128,1024]{2,1,0:T(8,128)(2,1)S(1)}, bf16[4,128,128]{2,1,0:T(8,128)(2,1)S(1)}) custom-call(bf16[512,128]{1,0:T(8,128)(2,1)} %bitcast.7, bf16[4,128,1024]{2,1,0:T(8,128)(2,1)} %enc_hbm.1, f32[4,1024]{1,0:T(4,128)} %bias_hbm.1, ...), custom_call_target="tpu_custom_call" | custom-call | tf_op jit(solution)/shard_map/transcoder/pallas_call | solution.py:246
  41.9 3.9 %weight_grads.1 = (f32[5,1024,256]{2,1,0:T(8,128)}, f32[4,128,1024]{2,1,0:T(8,128)}, f32[4,1024]{1,0:T(4,128)}) custom-call(bf16[4,128,1024]{2,1,0:T(8,128)(2,1)S(1)} %get-tuple-element.10.act_ref, bf16[8,2,16,256]{3,2,1,0:T(8,128)(2,1)S(1)} %get-tuple-element.11.res_ref, bf16[4,128,1024]{2,1,0:T(8,128)(2,1)S(1)} %get-tuple-element.12.pg_ref, ...), custom_call_target="tpu_custom_call" | custom-call | tf_op jit(solution)/shard_map/weight_grads/pallas_call | solution.py:313

commit v4 on v3

v4 whole, which is shorter than its diff:
```python
import jax
import jax.numpy as jnp
from jax import lax
from jax.experimental import pallas as pl
from jax.experimental.pallas import tpu as pltpu
from jax.sharding import PartitionSpec as P

MESH = pl.DeviceIdType.MESH
F32 = jnp.float32
BF16 = jnp.bfloat16
I32 = jnp.int32

TOKENS, LAYERS, TOPK, WIDTH, DIN, FEAT, BLOCKS, SLOTS = 128, 4, 64, 1024, 128, 256, 5, 8


def pick(values, lanes):
    return jnp.take_along_axis(values, lanes, axis=1, mode="promise_in_bounds")


def main_kernel(x_hbm, enc_hbm, bias_hbm, dec_hbm, dbias_hbm, tgt_hbm, idx_hbm,
                act_ref, res_ref, pg_ref, xt_ref,
                x_v, enc_v, bias_v, dec_v, dbias_v, tgt_v, idx_v, load_sem,
                xf, dense, inv, code_v, low_v, high_v, hot_a, hot_b, rows_v, val_v, pay_v, goal,
                ybuf, zbuf, lbuf, rs_src, rs_buf, hbuf, abuf,
                y_s, y_r, z_s, z_r, l_s, l_r, rs_s, rs_r, h_s, h_r, ag_s, ag_r):
    r = lax.axis_index("layer")
    j = lax.axis_index("lat")
    y = lax.rem(r, 4)
    zl = lax.div(r, 4)
    q = lax.rem(j, 8)
    zh = lax.div(j, 8)
    g = lax.div(r, 8)

    loads = [
        pltpu.make_async_copy(idx_hbm, idx_v, load_sem.at[0]),
        pltpu.make_async_copy(x_hbm, x_v, load_sem.at[1]),
        pltpu.make_async_copy(enc_hbm, enc_v, load_sem.at[2]),
        pltpu.make_async_copy(bias_hbm, bias_v, load_sem.at[3]),
        pltpu.make_async_copy(dec_hbm, dec_v, load_sem.at[4]),
        pltpu.make_async_copy(dbias_hbm, dbias_v, load_sem.at[5]),
        pltpu.make_async_copy(tgt_hbm.at[pl.ds(q * 16, 16)], tgt_v, load_sem.at[6]),
    ]
    for n in (0, 1, 2, 3, 5, 6):
        loads[n].start()

    def ypeer(i):
        return {"layer": zl * 4 + lax.rem(y + i, 4)}

    def zpeer(i):
        return {"layer": lax.rem(zl + i, 4) * 4 + y}

    def lpeer(i):
        return {"layer": lax.rem(r + i, 16)}

    def qpeer(i):
        return {"lat": zh * 8 + lax.rem(q + i, 8)}

    hpeer = {"lat": (1 - zh) * 8 + q}

    barrier = pltpu.get_barrier_semaphore()
    for i in range(1, 16):
        pl.semaphore_signal(barrier, inc=1, device_id=lpeer(i), device_id_type=MESH)
    for i in range(1, 8):
        pl.semaphore_signal(barrier, inc=1, device_id=qpeer(i), device_id_type=MESH)
    pl.semaphore_signal(barrier, inc=1, device_id=hpeer, device_id_type=MESH)

    lane16 = lax.broadcasted_iota(I32, (16, 128), 1)
    row16 = lax.broadcasted_iota(I32, (16, 128), 0)
    mine = (lane16 & 15) == row16

    loads[0].wait()
    tri = (lax.broadcasted_iota(I32, (TOPK, TOPK), 1)
           < lax.broadcasted_iota(I32, (TOPK, TOPK), 0)).astype(F32).astype(BF16)
    for l in range(LAYERS):
        local = idx_v[l] - j * WIDTH
        inside = (local >= 0) & (local < WIDTH)
        rank = jnp.dot(tri, inside.astype(F32).astype(BF16), preferred_element_type=F32)
        rank = jnp.where(inside, rank, -1.0)
        value = (local + 1).astype(F32)
        slots = []
        for s in range(SLOTS):
            row = jnp.sum(jnp.where(rank == float(s), value, 0.0), axis=0, keepdims=True)
            slots.append(jnp.broadcast_to(row, (16, 128)))
        code = jnp.transpose(jnp.concatenate(slots, axis=0)).astype(I32) - 1
        code_v[l] = code
        low_v[l] = code & 127
        high_v[l] = lax.shift_right_arithmetic(code, 7)

    loads[1].wait()
    loads[2].wait()
    loads[3].wait()
    loads[4].start()
    xf[...] = x_v[...].astype(F32)
    own = jnp.where(r == 0, 1.0, 0.0)
    for l in range(LAYERS):
        x_l = xf[pl.ds(l, TOKENS, stride=4), :]
        dense[l] = (jnp.dot(x_l.astype(BF16), enc_v[l], preferred_element_type=F32)
                    + bias_v[pl.ds(l, 1), :] * own)

    def gather(l, carry):
        own_lane = (lax.broadcasted_iota(I32, (TOKENS, 128), 1) & 15) == (
            lax.broadcasted_iota(I32, (TOKENS, 128), 0) & 15)
        low = low_v[l]
        high = high_v[l]
        got = jnp.zeros((TOKENS, 128), F32)
        for h in range(8):
            block = dense[l, :, pl.ds(h * 128, 128)]
            got = jnp.where(high == h, pick(block, low), got)
        got = jnp.where(own_lane, got, 0.0)
        ybuf[y, pl.ds(pl.multiple_of(l * 8, 8), 8), :] = jnp.sum(
            got.reshape(8, 16, 128), axis=1)
        return carry

    def scatter(out_ref):
        def step(b, carry):
            rows = pl.ds(pl.multiple_of(b * 16, 16), 16)
            for l in range(LAYERS):
                values = jnp.broadcast_to(val_v[pl.ds(l * 8 + b, 1), :], (16, 128))
                for h in range(8):
                    cols = pl.ds(h * 128, 128)
                    where = inv[l, rows, cols]
                    got = jnp.where(where >= 0, pick(values, where & 127), 0.0)
                    out_ref[l, rows, cols] = got.astype(BF16)
            return carry

        lax.fori_loop(0, 8, step, 0)

    def send(src, dst, s_sem, r_sem, peer):
        copy = pltpu.make_async_remote_copy(
            src_ref=src, dst_ref=dst, send_sem=s_sem, recv_sem=r_sem,
            device_id=peer, device_id_type=MESH)
        copy.start()
        return copy

    def arrive(buf, other, s_sem, r_sem, peer):
        pltpu.make_async_remote_copy(
            src_ref=buf.at[other], dst_ref=buf.at[other], send_sem=s_sem,
            recv_sem=r_sem, device_id=peer, device_id_type=MESH).wait_recv()

    def exchange(buf, me, n, peer, s_sem, r_sem, between=None):
        sends = [send(buf.at[me], buf.at[me], s_sem.at[i], r_sem.at[me], peer(i))
                 for i in range(n - 1, 0, -1)]
        if between is not None:
            between()
        for i in range(1, n):
            other = lax.rem(me + i, n)
            arrive(buf, other, s_sem.at[i], r_sem.at[other], peer(i))
        for copy in sends:
            copy.wait_send()

    def total(buf, n):
        acc = buf[0].astype(F32)
        for i in range(1, n):
            acc = acc + buf[i].astype(F32)
        return acc

    def source_of(k):
        return jnp.where(k <= g, k, k - g - 1)

    def gather_decoder(begin, end):

        def build(hot, b):
            tokens = pl.ds(pl.multiple_of(b * 16, 16), 16)
            for l in range(LAYERS):
                code = code_v[l, tokens, :]
                for s in range(SLOTS):
                    at = jnp.broadcast_to(code[:, s * 16:s * 16 + 1], (16, 128))
                    for h in range(8):
                        hot[l, pl.ds(s * 16, 16), pl.ds(h * 128, 128)] = jnp.where(
                            at == lane16 + h * 128, 1.0, 0.0).astype(BF16)

        def multiply(hot, b):
            for k in range(BLOCKS):
                rows_v[b, pl.ds(k * 128, 128), :] = jnp.dot(
                    hot[source_of(k)], dec_v[k], preferred_element_type=F32).astype(BF16)

        def step(n, carry):
            build(hot_b, 2 * n + 1)
            multiply(hot_a, 2 * n)
            build(hot_a, jnp.minimum(2 * n + 2, 7))
            multiply(hot_b, 2 * n + 1)
            return carry

        if begin == 0:
            loads[4].wait()
            build(hot_a, 0)
        lax.fori_loop(begin, end, step, 0)

    def build_inverse():
        def step(b, carry):
            tokens = pl.ds(pl.multiple_of(b * 16, 16), 16)
            for l in range(LAYERS):
                code = code_v[l, tokens, :]
                found = [jnp.full((16, 128), -1, I32) for h in range(8)]
                for s in range(SLOTS):
                    at = jnp.broadcast_to(code[:, s * 16:s * 16 + 1], (16, 128))
                    for h in range(8):
                        found[h] = jnp.where(at == lane16 + h * 128, row16 + s * 16, found[h])
                for h in range(8):
                    inv[l, tokens, pl.ds(h * 128, 128)] = found[h]
            return carry

        lax.fori_loop(0, 8, step, 0)

    def prepare():
        gather_decoder(2, 4)
        for l in range(LAYERS):
            xt_ref[l] = jnp.transpose(xf[pl.ds(l, TOKENS, stride=4), :]).astype(BF16)
        loads[5].wait()
        loads[6].wait()
        goal_all = tgt_v[...].astype(F32)
        for c in range(2):
            goal[c] = goal_all[:, c, :]

    lax.fori_loop(0, LAYERS, gather, 0)
    pl.semaphore_wait(barrier, 23)
    exchange(ybuf, y, 4, ypeer, y_s, y_r, between=lambda: gather_decoder(0, 2))
    zbuf[zl] = total(ybuf, 4)
    exchange(zbuf, zl, 4, zpeer, z_s, z_r, between=prepare)
    val_v[...] = total(zbuf, 4).astype(BF16).astype(F32)

    def rebuild(b):
        zero = jnp.zeros((16, 128), F32)
        top, bottom = [], []
        for k in range(BLOCKS):
            row = val_v[pl.ds(source_of(k) * 8 + b, 1), :]
            block = jnp.where(mine, jnp.broadcast_to(row, (16, 128)), 0.0)
            if k == 0:
                top.append(block)
                bottom.append(zero)
            elif k == 1:
                top.append(block * jnp.where(g == 1, 1.0, 0.0))
                bottom.append(block * jnp.where(g == 1, 0.0, 1.0))
            else:
                top.append(zero)
                bottom.append(block)
        left = jnp.concatenate([jnp.concatenate(top, axis=1), jnp.concatenate(bottom, axis=1)],
                               axis=0)
        return jnp.dot(left.astype(BF16), rows_v[b],
                       preferred_element_type=F32).reshape(2, 16, FEAT)

    def give(i):
        other = lax.rem(q + i, 8)
        return send(rs_src.at[other], rs_buf.at[q], rs_s.at[i], rs_r.at[q], qpeer(i))

    order = (4, 3, 5, 2, 6, 1, 7)
    sends = []
    for n, i in enumerate(order):
        b = lax.rem(q + i, 8)
        rs_src[b] = rebuild(b).astype(BF16)
        if n > 0:
            sends.append(give(order[n - 1]))
    rs_buf[q] = rebuild(q).astype(BF16)
    sends.append(give(order[-1]))
    build_inverse()
    for i in range(1, 8):
        other = lax.rem(q + i, 8)
        arrive(rs_buf, other, rs_s.at[i], rs_r.at[other], qpeer(i))
    hbuf[zh] = total(rs_buf, 8)
    copy = send(hbuf.at[zh], hbuf.at[zh], h_s, h_r.at[zh], hpeer)
    scatter(act_ref)
    for other in sends:
        other.wait_send()
    arrive(hbuf, 1 - zh, h_s, h_r.at[1 - zh], hpeer)
    copy.wait_send()
    rebuilt = total(hbuf, 2)
    for c in range(2):
        abuf[q, c] = (rebuilt[c] + dbias_v[pl.ds(c, 1), :] - goal[c]).astype(BF16)

    def back(b):
        out = lax.dot_general(abuf[b].reshape(32, FEAT), rows_v[b], (((1,), (1,)), ((), ())),
                              preferred_element_type=F32)

        def part(c, k):
            block = out[c * 16:c * 16 + 16, k * 128:k * 128 + 128]
            return jnp.sum(jnp.where(mine, block, 0.0), axis=0, keepdims=True)

        p0 = part(0, 0)
        p1 = jnp.where(g == 1, part(0, 1), part(1, 1))
        p2, p3, p4 = part(1, 2), part(1, 3), part(1, 4)
        pay_v[pl.ds(b, 1), :] = p0 + jnp.where(g == 1, p2, p1)
        pay_v[pl.ds(8 + b, 1), :] = jnp.where(g == 1, p1 + p3, p2)
        pay_v[pl.ds(16 + b, 1), :] = jnp.where(g == 1, p4, p3)
        pay_v[pl.ds(24 + b, 1), :] = jnp.where(g == 1, jnp.zeros_like(p4), p4)

    sends = [send(abuf.at[q], abuf.at[q], ag_s.at[i], ag_r.at[q], qpeer(i)) for i in order]
    back(q)
    for i in (1, 7, 2, 6, 3, 5, 4):
        other = lax.rem(q + i, 8)
        arrive(abuf, other, ag_s.at[i], ag_r.at[other], qpeer(i))
        back(other)
    for copy in sends:
        copy.wait_send()
    lbuf[r] = pay_v[...].astype(BF16)

    def keep_residue():
        res_ref[...] = abuf[...]

    exchange(lbuf, r, 16, lpeer, l_s, l_r, between=keep_residue)
    val_v[...] = total(lbuf, 16).astype(BF16).astype(F32)
    scatter(pg_ref)


def main_call(x, enc, bias, dec, dbias, tgt, idx):
    dma = pltpu.SemaphoreType.DMA
    vmem = pltpu.VMEM
    return pl.pallas_call(
        main_kernel,
        out_shape=(
            jax.ShapeDtypeStruct((LAYERS, TOKENS, WIDTH), BF16),
            jax.ShapeDtypeStruct((8, 2, 16, FEAT), BF16),
            jax.ShapeDtypeStruct((LAYERS, TOKENS, WIDTH), BF16),
            jax.ShapeDtypeStruct((LAYERS, DIN, TOKENS), BF16),
        ),
        in_specs=[pl.BlockSpec(memory_space=pltpu.HBM)] * 7,
        out_specs=(pl.BlockSpec(memory_space=pltpu.VMEM),) * 4,
        scratch_shapes=[
            vmem((TOKENS * LAYERS, DIN), BF16),
            vmem((LAYERS, DIN, WIDTH), BF16),
            vmem((LAYERS, WIDTH), F32),
            vmem((BLOCKS, WIDTH, FEAT), BF16),
            vmem((2, FEAT), F32),
            vmem((16, 2, FEAT), BF16),
            vmem((LAYERS, TOPK, TOKENS), I32),
            dma((7,)),
            vmem((TOKENS * LAYERS, DIN), F32),
            vmem((LAYERS, TOKENS, WIDTH), F32),
            vmem((LAYERS, TOKENS, WIDTH), I32),
            vmem((LAYERS, TOKENS, 128), I32),
            vmem((LAYERS, TOKENS, 128), I32),
            vmem((LAYERS, TOKENS, 128), I32),
            vmem((LAYERS, 128, WIDTH), BF16),
            vmem((LAYERS, 128, WIDTH), BF16),
            vmem((8, BLOCKS * 128, FEAT), BF16),
            vmem((32, 128), F32),
            vmem((32, 128), F32),
            vmem((2, 16, FEAT), F32),
            vmem((4, 32, 128), F32),
            vmem((4, 32, 128), F32),
            vmem((16, 32, 128), BF16),
            vmem((8, 2, 16, FEAT), BF16),
            vmem((8, 2, 16, FEAT), BF16),
            vmem((2, 2, 16, FEAT), F32),
            vmem((8, 2, 16, FEAT), BF16),
            dma((4,)), dma((4,)), dma((4,)), dma((4,)), dma((16,)), dma((16,)),
            dma((8,)), dma((8,)), dma, dma((2,)), dma((8,)), dma((8,)),
        ],
        compiler_params=pltpu.CompilerParams(collective_id=0, has_side_effects=True,
                                             vmem_limit_bytes=28 * 2**20),
        name="transcoder",
    )(*[pltpu.with_memory_space_constraint(v, pltpu.HBM)
        for v in (x, enc, bias, dec, dbias, tgt, idx)])


def grad_kernel(act_ref, res_ref, pg_ref, xt_ref, dg_hbm, eg_hbm, bg_ref, dg_v, eg_v, sem):
    g = lax.div(lax.axis_index("layer"), 8)
    copies = []
    for k in range(LAYERS):
        eg_v[k] = jnp.dot(xt_ref[k], pg_ref[k], preferred_element_type=F32)
        copies.append(pltpu.make_async_copy(eg_v.at[k], eg_hbm.at[k], sem.at[BLOCKS + k]))
        copies[-1].start()
    for k in range(BLOCKS):
        source = jnp.where(k <= g, k, k - g - 1)
        slot = jnp.where(k <= g, 0, 1)
        residue = res_ref[:, slot].reshape(TOKENS, FEAT)
        dg_v[k] = lax.dot_general(act_ref[source], residue, (((0,), (0,)), ((), ())),
                                  preferred_element_type=F32)
        copies.append(pltpu.make_async_copy(dg_v.at[k], dg_hbm.at[k], sem.at[k]))
        copies[-1].start()
    for k in range(LAYERS):
        bg_ref[pl.ds(k, 1), :] = jnp.dot(jnp.ones((8, TOKENS), BF16), pg_ref[k],
                                         preferred_element_type=F32)[0:1]
    for copy in copies:
        copy.wait()


def grad_call(act, res, pg, xt):
    vmem = pltpu.VMEM
    return pl.pallas_call(
        grad_kernel,
        out_shape=(
            jax.ShapeDtypeStruct((BLOCKS, WIDTH, FEAT), F32),
            jax.ShapeDtypeStruct((LAYERS, DIN, WIDTH), F32),
            jax.ShapeDtypeStruct((LAYERS, WIDTH), F32),
        ),
        in_specs=[pl.BlockSpec(memory_space=vmem)] * 4,
        out_specs=(pl.BlockSpec(memory_space=pl.ANY), pl.BlockSpec(memory_space=pl.ANY),
                   pl.BlockSpec(memory_space=vmem)),
        scratch_shapes=[vmem((BLOCKS, WIDTH, FEAT), F32), vmem((LAYERS, DIN, WIDTH), F32),
                        pltpu.SemaphoreType.DMA((BLOCKS + LAYERS,))],
        compiler_params=pltpu.CompilerParams(vmem_limit_bytes=24 * 2**20),
        name="weight_grads",
    )(act, res, pg, xt)


def body(inputs, encoder, enc_bias, decoder, dec_bias, targets, top_index):
    act, res, pg, xt = main_call(
        inputs.reshape(TOKENS * LAYERS, DIN), encoder, enc_bias, decoder[0], dec_bias[0],
        targets[0], jnp.transpose(top_index, (1, 2, 0)))
    dg, eg, bg = grad_call(act, res, pg, xt)
    return dg[None], eg, bg


def solution(mesh):
    return jax.shard_map(
        body,
        mesh=mesh,
        in_specs=(
            P(None, None, "layer"),
            P(None, "layer", "lat"),
            P(None, "lat"),
            P("layer", None, "lat", None),
            P("layer", None, None),
            P("layer", None, None, None),
            P(),
        ),
        out_specs=(P("layer", None, "lat", None), P(None, "layer", "lat"), P(None, "lat")),
        check_vma=False,
    )
```

time: 45.9 us -> 45.4 us (0.989)
  Pallas kernels: 45.2 us -> 44.7 us
    pallas_call x1, Pallas kernels: 41.3 us -> 40.8 us  [main_call(): pl.pallas_call(main_kernel, out_shape=(jax.ShapeDtypeStruct((LAYERS, TOKE...]
where the time goes in v4:
time: 45.4 us; the launch traced here: 45.3 us
  Pallas kernels  44.7 us (98%)
  between operations  0.64 us (1%)
    pallas_call x1, Pallas kernels, main_call(): pl.pallas_call(main_kernel, out_shape=(jax.ShapeDtypeStruct((LAYERS, TOKE...  40.8 us
    pallas_call x1, Pallas kernels, grad_call(): pl.pallas_call(grad_kernel, out_shape=(jax.ShapeDtypeStruct((BLOCKS, WIDT...  3.88 us

profile of v4, /device:TPU:1, one launch (start us, length us, event | category | flops | bytes accessed | tf_op | source)
XLA Modules:
  0.0 45.3 jit_solution(11669108861494740198)
XLA Ops:
  0.6 40.8 %transcoder.1 = (bf16[4,128,1024]{2,1,0:T(8,128)(2,1)S(1)}, bf16[8,2,16,256]{3,2,1,0:T(8,128)(2,1)S(1)}, bf16[4,128,1024]{2,1,0:T(8,128)(2,1)S(1)}, bf16[4,128,128]{2,1,0:T(8,128)(2,1)S(1)}) custom-call(bf16[512,128]{1,0:T(8,128)(2,1)} %bitcast.7, bf16[4,128,1024]{2,1,0:T(8,128)(2,1)} %enc_hbm.1, f32[4,1024]{1,0:T(4,128)} %bias_hbm.1, ...), custom_call_target="tpu_custom_call" | custom-call | tf_op jit(solution)/shard_map/transcoder/pallas_call | solution.py:307
  41.4 3.9 %weight_grads.1 = (f32[5,1024,256]{2,1,0:T(8,128)}, f32[4,128,1024]{2,1,0:T(8,128)}, f32[4,1024]{1,0:T(4,128)}) custom-call(bf16[4,128,1024]{2,1,0:T(8,128)(2,1)S(1)} %get-tuple-element.10.act_ref, bf16[8,2,16,256]{3,2,1,0:T(8,128)(2,1)S(1)} %get-tuple-element.11.res_ref, bf16[4,128,1024]{2,1,0:T(8,128)(2,1)S(1)} %get-tuple-element.12.pg_ref, ...), custom_call_target="tpu_custom_call" | custom-call | tf_op jit(solution)/shard_map/weight_grads/pallas_call | solution.py:379

commit v5 on v4

--- a/solution.py
+++ b/solution.py
@@ -17,10 +17,20 @@
     return jnp.take_along_axis(values, lanes, axis=1, mode="promise_in_bounds")
 
 
+def scatter(out_ref, values_ref, inv_ref, l, b):
+    rows = pl.ds(pl.multiple_of(b * 16, 16), 16)
+    values = jnp.broadcast_to(values_ref[pl.ds(l * 8 + b, 1), :], (16, 128))
+    for h in range(8):
+        cols = pl.ds(h * 128, 128)
+        where = inv_ref[l, rows, cols]
+        got = jnp.where(where >= 0, pick(values, where & 127), 0.0)
+        out_ref[l, rows, cols] = got.astype(BF16)
+
+
 def main_kernel(x_hbm, enc_hbm, bias_hbm, dec_hbm, dbias_hbm, tgt_hbm, idx_hbm,
-                act_ref, res_ref, pg_ref, xt_ref,
+                act_ref, res_ref, pick_ref, inv, xt_ref,
                 x_v, enc_v, bias_v, dec_v, dbias_v, tgt_v, idx_v, load_sem,
-                xf, dense, inv, code_v, low_v, high_v, hot_a, hot_b, rows_v, val_v, pay_v, goal,
+                xf, dense, code_v, low_v, high_v, hot_a, hot_b, rows_v, val_v, pay_v, goal,
                 ybuf, zbuf, lbuf, rs_src, rs_buf, hbuf, abuf,
                 y_s, y_r, z_s, z_r, l_s, l_r, rs_s, rs_r, h_s, h_r, ag_s, ag_r):
     r = lax.axis_index("layer")
@@ -110,20 +120,6 @@
         ybuf[y, pl.ds(pl.multiple_of(l * 8, 8), 8), :] = jnp.sum(
             got.reshape(8, 16, 128), axis=1)
         return carry
-
-    def scatter(out_ref):
-        def step(b, carry):
-            rows = pl.ds(pl.multiple_of(b * 16, 16), 16)
-            for l in range(LAYERS):
-                values = jnp.broadcast_to(val_v[pl.ds(l * 8 + b, 1), :], (16, 128))
-                for h in range(8):
-                    cols = pl.ds(h * 128, 128)
-                    where = inv[l, rows, cols]
-                    got = jnp.where(where >= 0, pick(values, where & 127), 0.0)
-                    out_ref[l, rows, cols] = got.astype(BF16)
-            return carry
-
-        lax.fori_loop(0, 8, step, 0)
 
     def send(src, dst, s_sem, r_sem, peer):
         copy = pltpu.make_async_remote_copy(
@@ -256,9 +252,14 @@
     for i in range(1, 8):
         other = lax.rem(q + i, 8)
         arrive(rs_buf, other, rs_s.at[i], rs_r.at[other], qpeer(i))
-    hbuf[zh] = total(rs_buf, 8)
+    hbuf[zh] = total(rs_buf, 8).astype(BF16)
     copy = send(hbuf.at[zh], hbuf.at[zh], h_s, h_r.at[zh], hpeer)
-    scatter(act_ref)
+    def spread(b, carry):
+        for l in range(LAYERS):
+            scatter(act_ref, val_v, inv, l, b)
+        return carry
+
+    lax.fori_loop(0, 8, spread, 0)
     for other in sends:
         other.wait_send()
     arrive(hbuf, 1 - zh, h_s, h_r.at[1 - zh], hpeer)
@@ -297,8 +298,7 @@
         res_ref[...] = abuf[...]
 
     exchange(lbuf, r, 16, lpeer, l_s, l_r, between=keep_residue)
-    val_v[...] = total(lbuf, 16).astype(BF16).astype(F32)
-    scatter(pg_ref)
+    pick_ref[...] = total(lbuf, 16).astype(BF16).astype(F32)
 
 
 def main_call(x, enc, bias, dec, dbias, tgt, idx):
@@ -309,11 +309,12 @@
         out_shape=(
             jax.ShapeDtypeStruct((LAYERS, TOKENS, WIDTH), BF16),
             jax.ShapeDtypeStruct((8, 2, 16, FEAT), BF16),
-            jax.ShapeDtypeStruct((LAYERS, TOKENS, WIDTH), BF16),
+            jax.ShapeDtypeStruct((32, 128), F32),
+            jax.ShapeDtypeStruct((LAYERS, TOKENS, WIDTH), I32),
             jax.ShapeDtypeStruct((LAYERS, DIN, TOKENS), BF16),
         ),
         in_specs=[pl.BlockSpec(memory_space=pltpu.HBM)] * 7,
-        out_specs=(pl.BlockSpec(memory_space=pltpu.VMEM),) * 4,
+        out_specs=(pl.BlockSpec(memory_space=pltpu.VMEM),) * 5,
         scratch_shapes=[
             vmem((TOKENS * LAYERS, DIN), BF16),
             vmem((LAYERS, DIN, WIDTH), BF16),
@@ -325,7 +326,6 @@
             dma((7,)),
             vmem((TOKENS * LAYERS, DIN), F32),
             vmem((LAYERS, TOKENS, WIDTH), F32),
-            vmem((LAYERS, TOKENS, WIDTH), I32),
             vmem((LAYERS, TOKENS, 128), I32),
             vmem((LAYERS, TOKENS, 128), I32),
             vmem((LAYERS, TOKENS, 128), I32),
@@ -340,7 +340,7 @@
             vmem((16, 32, 128), BF16),
             vmem((8, 2, 16, FEAT), BF16),
             vmem((8, 2, 16, FEAT), BF16),
-            vmem((2, 2, 16, FEAT), F32),
+            vmem((2, 2, 16, FEAT), BF16),
             vmem((8, 2, 16, FEAT), BF16),
             dma((4,)), dma((4,)), dma((4,)), dma((4,)), dma((16,)), dma((16,)),
             dma((8,)), dma((8,)), dma, dma((2,)), dma((8,)), dma((8,)),
@@ -352,13 +352,10 @@
         for v in (x, enc, bias, dec, dbias, tgt, idx)])
 
 
-def grad_kernel(act_ref, res_ref, pg_ref, xt_ref, dg_hbm, eg_hbm, bg_ref, dg_v, eg_v, sem):
+def grad_kernel(act_ref, res_ref, pick_ref, inv_ref, xt_ref, dg_hbm, eg_hbm, bg_ref,
+                dg_v, eg_v, pg_v, sem):
     g = lax.div(lax.axis_index("layer"), 8)
     copies = []
-    for k in range(LAYERS):
-        eg_v[k] = jnp.dot(xt_ref[k], pg_ref[k], preferred_element_type=F32)
-        copies.append(pltpu.make_async_copy(eg_v.at[k], eg_hbm.at[k], sem.at[BLOCKS + k]))
-        copies[-1].start()
     for k in range(BLOCKS):
         source = jnp.where(k <= g, k, k - g - 1)
         slot = jnp.where(k <= g, 0, 1)
@@ -367,14 +364,24 @@
                                   preferred_element_type=F32)
         copies.append(pltpu.make_async_copy(dg_v.at[k], dg_hbm.at[k], sem.at[k]))
         copies[-1].start()
-    for k in range(LAYERS):
-        bg_ref[pl.ds(k, 1), :] = jnp.dot(jnp.ones((8, TOKENS), BF16), pg_ref[k],
+    def layer(l, carry):
+        for b in range(8):
+            scatter(pg_v, pick_ref, inv_ref, l, b)
+        grads = pg_v[l]
+        eg_v[l] = jnp.dot(xt_ref[l], grads, preferred_element_type=F32)
+        pltpu.make_async_copy(eg_v.at[l], eg_hbm.at[l], sem.at[BLOCKS + l]).start()
+        bg_ref[pl.ds(l, 1), :] = jnp.dot(jnp.ones((8, TOKENS), BF16), grads,
                                          preferred_element_type=F32)[0:1]
+        return carry
+
+    lax.fori_loop(0, LAYERS, layer, 0)
+    for l in range(LAYERS):
+        pltpu.make_async_copy(eg_v.at[l], eg_hbm.at[l], sem.at[BLOCKS + l]).wait()
     for copy in copies:
         copy.wait()
 
 
-def grad_call(act, res, pg, xt):
+def grad_call(act, res, picked, inv, xt):
     vmem = pltpu.VMEM
     return pl.pallas_call(
         grad_kernel,
@@ -383,21 +390,22 @@
             jax.ShapeDtypeStruct((LAYERS, DIN, WIDTH), F32),
             jax.ShapeDtypeStruct((LAYERS, WIDTH), F32),
         ),
-        in_specs=[pl.BlockSpec(memory_space=vmem)] * 4,
+        in_specs=[pl.BlockSpec(memory_space=vmem)] * 5,
         out_specs=(pl.BlockSpec(memory_space=pl.ANY), pl.BlockSpec(memory_space=pl.ANY),
                    pl.BlockSpec(memory_space=vmem)),
         scratch_shapes=[vmem((BLOCKS, WIDTH, FEAT), F32), vmem((LAYERS, DIN, WIDTH), F32),
+                        vmem((LAYERS, TOKENS, WIDTH), BF16),
                         pltpu.SemaphoreType.DMA((BLOCKS + LAYERS,))],
         compiler_params=pltpu.CompilerParams(vmem_limit_bytes=24 * 2**20),
         name="weight_grads",
-    )(act, res, pg, xt)
+    )(act, res, picked, inv, xt)
 
 
 def body(inputs, encoder, enc_bias, decoder, dec_bias, targets, top_index):
-    act, res, pg, xt = main_call(
+    act, res, picked, inv, xt = main_call(
         inputs.reshape(TOKENS * LAYERS, DIN), encoder, enc_bias, decoder[0], dec_bias[0],
         targets[0], jnp.transpose(top_index, (1, 2, 0)))
-    dg, eg, bg = grad_call(act, res, pg, xt)
+    dg, eg, bg = grad_call(act, res, picked, inv, xt)
     return dg[None], eg, bg
 
 

time: 45.4 us -> 43.9 us (0.967)
  Pallas kernels: 44.7 us -> 43.1 us
    pallas_call x1, Pallas kernels: 40.8 us -> 37.8 us  [main_call(): pl.pallas_call(main_kernel, out_shape=(jax.ShapeDtypeStruct((LAYERS, TOKE...]
    pallas_call x1, Pallas kernels: 3.88 us -> 5.34 us  [grad_call(): pl.pallas_call(grad_kernel, out_shape=(jax.ShapeDtypeStruct((BLOCKS, WIDT...]
where the time goes in v5:
time: 43.9 us; the launch traced here: 43.8 us
  Pallas kernels  43.1 us (98%)
  between operations  0.64 us (1%)
    pallas_call x1, Pallas kernels, main_call(): pl.pallas_call(main_kernel, out_shape=(jax.ShapeDtypeStruct((LAYERS, TOKE...  37.8 us
    pallas_call x1, Pallas kernels, grad_call(): pl.pallas_call(grad_kernel, out_shape=(jax.ShapeDtypeStruct((BLOCKS, WIDT...  5.34 us

profile of v5, /device:TPU:1, one launch (start us, length us, event | category | flops | bytes accessed | tf_op | source)
XLA Modules:
  0.0 43.8 jit_solution(9493888329839210761)
XLA Ops:
  0.6 37.8 %transcoder.1 = (bf16[4,128,1024]{2,1,0:T(8,128)(2,1)S(1)}, bf16[8,2,16,256]{3,2,1,0:T(8,128)(2,1)S(1)}, f32[32,128]{1,0:T(8,128)S(1)}, s32[4,128,1024]{2,1,0:T(8,128)S(1)}, bf16[4,128,128]{2,1,0:T(8,128)(2,1)S(1)}) custom-call(bf16[512,128]{1,0:T(8,128)(2,1)} %bitcast.7, bf16[4,128,1024]{2,1,0:T(8,128)(2,1)} %enc_hbm.1, f32[4,1024]{1,0:T(4,128)} %bias_hbm.1, ...), custom_call_target="tpu_custom_call" | custom-call | tf_op jit(solution)/shard_map/transcoder/pallas_call | solution.py:307
  38.4 5.3 %weight_grads.1 = (f32[5,1024,256]{2,1,0:T(8,128)}, f32[4,128,1024]{2,1,0:T(8,128)}, f32[4,1024]{1,0:T(4,128)}) custom-call(bf16[4,128,1024]{2,1,0:T(8,128)(2,1)S(1)} %get-tuple-element.11.act_ref, bf16[8,2,16,256]{3,2,1,0:T(8,128)(2,1)S(1)} %get-tuple-element.12.res_ref, f32[32,128]{1,0:T(8,128)S(1)} %get-tuple-element.13.pick_ref, ...), custom_call_target="tpu_custom_call" | custom-call | tf_op jit(solution)/shard_map/weight_grads/pallas_call | solution.py:386

commit v6 on v5

--- a/solution.py
+++ b/solution.py
@@ -28,10 +28,10 @@
 
 
 def main_kernel(x_hbm, enc_hbm, bias_hbm, dec_hbm, dbias_hbm, tgt_hbm, idx_hbm,
-                act_ref, res_ref, pick_ref, inv, xt_ref,
+                dg_ref, pick_ref, inv, xt_ref,
                 x_v, enc_v, bias_v, dec_v, dbias_v, tgt_v, idx_v, load_sem,
                 xf, dense, code_v, low_v, high_v, hot_a, hot_b, rows_v, val_v, pay_v, goal,
-                ybuf, zbuf, lbuf, rs_src, rs_buf, hbuf, abuf,
+                act_v, ybuf, zbuf, lbuf, rs_src, rs_buf, hbuf, abuf,
                 y_s, y_r, z_s, z_r, l_s, l_r, rs_s, rs_r, h_s, h_r, ag_s, ag_r):
     r = lax.axis_index("layer")
     j = lax.axis_index("lat")
@@ -256,7 +256,7 @@
     copy = send(hbuf.at[zh], hbuf.at[zh], h_s, h_r.at[zh], hpeer)
     def spread(b, carry):
         for l in range(LAYERS):
-            scatter(act_ref, val_v, inv, l, b)
+            scatter(act_v, val_v, inv, l, b)
         return carry
 
     lax.fori_loop(0, 8, spread, 0)
@@ -294,10 +294,13 @@
         copy.wait_send()
     lbuf[r] = pay_v[...].astype(BF16)
 
-    def keep_residue():
-        res_ref[...] = abuf[...]
-
-    exchange(lbuf, r, 16, lpeer, l_s, l_r, between=keep_residue)
+    def decoder_grads():
+        for k in range(BLOCKS):
+            residue = abuf[:, jnp.where(k <= g, 0, 1)].reshape(TOKENS, FEAT)
+            dg_ref[k] = lax.dot_general(act_v[source_of(k)], residue, (((0,), (0,)), ((), ())),
+                                        preferred_element_type=F32)
+
+    exchange(lbuf, r, 16, lpeer, l_s, l_r, between=decoder_grads)
     pick_ref[...] = total(lbuf, 16).astype(BF16).astype(F32)
 
 
@@ -307,14 +310,13 @@
     return pl.pallas_call(
         main_kernel,
         out_shape=(
-            jax.ShapeDtypeStruct((LAYERS, TOKENS, WIDTH), BF16),
-            jax.ShapeDtypeStruct((8, 2, 16, FEAT), BF16),
+            jax.ShapeDtypeStruct((BLOCKS, WIDTH, FEAT), F32),
             jax.ShapeDtypeStruct((32, 128), F32),
             jax.ShapeDtypeStruct((LAYERS, TOKENS, WIDTH), I32),
             jax.ShapeDtypeStruct((LAYERS, DIN, TOKENS), BF16),
         ),
         in_specs=[pl.BlockSpec(memory_space=pltpu.HBM)] * 7,
-        out_specs=(pl.BlockSpec(memory_space=pltpu.VMEM),) * 5,
+        out_specs=(pl.BlockSpec(memory_space=pltpu.VMEM),) * 4,
         scratch_shapes=[
             vmem((TOKENS * LAYERS, DIN), BF16),
             vmem((LAYERS, DIN, WIDTH), BF16),
@@ -335,6 +337,7 @@
             vmem((32, 128), F32),
             vmem((32, 128), F32),
             vmem((2, 16, FEAT), F32),
+            vmem((LAYERS, TOKENS, WIDTH), BF16),
             vmem((4, 32, 128), F32),
             vmem((4, 32, 128), F32),
             vmem((16, 32, 128), BF16),
@@ -352,18 +355,12 @@
         for v in (x, enc, bias, dec, dbias, tgt, idx)])
 
 
-def grad_kernel(act_ref, res_ref, pick_ref, inv_ref, xt_ref, dg_hbm, eg_hbm, bg_ref,
-                dg_v, eg_v, pg_v, sem):
-    g = lax.div(lax.axis_index("layer"), 8)
-    copies = []
-    for k in range(BLOCKS):
-        source = jnp.where(k <= g, k, k - g - 1)
-        slot = jnp.where(k <= g, 0, 1)
-        residue = res_ref[:, slot].reshape(TOKENS, FEAT)
-        dg_v[k] = lax.dot_general(act_ref[source], residue, (((0,), (0,)), ((), ())),
-                                  preferred_element_type=F32)
-        copies.append(pltpu.make_async_copy(dg_v.at[k], dg_hbm.at[k], sem.at[k]))
-        copies[-1].start()
+def grad_kernel(dg_ref, pick_ref, inv_ref, xt_ref, dg_hbm, eg_hbm, bg_ref, eg_v, pg_v, sem):
+    copies = [pltpu.make_async_copy(dg_ref.at[k], dg_hbm.at[k], sem.at[k])
+              for k in range(BLOCKS)]
+    for copy in copies:
+        copy.start()
+
     def layer(l, carry):
         for b in range(8):
             scatter(pg_v, pick_ref, inv_ref, l, b)
@@ -381,7 +378,7 @@
         copy.wait()
 
 
-def grad_call(act, res, picked, inv, xt):
+def grad_call(dg, picked, inv, xt):
     vmem = pltpu.VMEM
     return pl.pallas_call(
         grad_kernel,
@@ -390,22 +387,22 @@
             jax.ShapeDtypeStruct((LAYERS, DIN, WIDTH), F32),
             jax.ShapeDtypeStruct((LAYERS, WIDTH), F32),
         ),
-        in_specs=[pl.BlockSpec(memory_space=vmem)] * 5,
+        in_specs=[pl.BlockSpec(memory_space=vmem)] * 4,
         out_specs=(pl.BlockSpec(memory_space=pl.ANY), pl.BlockSpec(memory_space=pl.ANY),
                    pl.BlockSpec(memory_space=vmem)),
-        scratch_shapes=[vmem((BLOCKS, WIDTH, FEAT), F32), vmem((LAYERS, DIN, WIDTH), F32),
+        scratch_shapes=[vmem((LAYERS, DIN, WIDTH), F32),
                         vmem((LAYERS, TOKENS, WIDTH), BF16),
                         pltpu.SemaphoreType.DMA((BLOCKS + LAYERS,))],
         compiler_params=pltpu.CompilerParams(vmem_limit_bytes=24 * 2**20),
         name="weight_grads",
-    )(act, res, picked, inv, xt)
+    )(dg, picked, inv, xt)
 
 
 def body(inputs, encoder, enc_bias, decoder, dec_bias, targets, top_index):
-    act, res, picked, inv, xt = main_call(
+    dg, picked, inv, xt = main_call(
         inputs.reshape(TOKENS * LAYERS, DIN), encoder, enc_bias, decoder[0], dec_bias[0],
         targets[0], jnp.transpose(top_index, (1, 2, 0)))
-    dg, eg, bg = grad_call(act, res, picked, inv, xt)
+    dg, eg, bg = grad_call(dg, picked, inv, xt)
     return dg[None], eg, bg
 
 

time: 43.9 us -> 42.9 us (0.977)
  Pallas kernels: 43.1 us -> 42.1 us
    pallas_call x1, Pallas kernels: 5.34 us -> 4.31 us  [grad_call(): pl.pallas_call(grad_kernel, out_shape=(jax.ShapeDtypeStruct((BLOCKS, WIDT...]
where the time goes in v6:
time: 42.9 us; the launch traced here: 42.8 us
  Pallas kernels  42.1 us (98%)
  between operations  0.64 us (1%)
    pallas_call x1, Pallas kernels, main_call(): pl.pallas_call(main_kernel, out_shape=(jax.ShapeDtypeStruct((BLOCKS, WIDT...  37.8 us
    pallas_call x1, Pallas kernels, grad_call(): pl.pallas_call(grad_kernel, out_shape=(jax.ShapeDtypeStruct((BLOCKS, WIDT...  4.31 us

profile of v6, /device:TPU:1, one launch (start us, length us, event | category | flops | bytes accessed | tf_op | source)
XLA Modules:
  0.0 42.8 jit_solution(10955593229020103652)
XLA Ops:
  0.6 37.8 %transcoder.1 = (f32[5,1024,256]{2,1,0:T(8,128)S(1)}, f32[32,128]{1,0:T(8,128)S(1)}, s32[4,128,1024]{2,1,0:T(8,128)S(1)}, bf16[4,128,128]{2,1,0:T(8,128)(2,1)S(1)}) custom-call(bf16[512,128]{1,0:T(8,128)(2,1)} %bitcast.7, bf16[4,128,1024]{2,1,0:T(8,128)(2,1)} %enc_hbm.1, f32[4,1024]{1,0:T(4,128)} %bias_hbm.1, bf16[5,1024,256]{2,1,0:T(8,128)(2,1)} %bitcast.6, ...), custom_call_target="tpu_custom_call" | custom-call | tf_op jit(solution)/shard_map/transcoder/pallas_call | solution.py:310
  38.4 4.3 %weight_grads.1 = (f32[5,1024,256]{2,1,0:T(8,128)}, f32[4,128,1024]{2,1,0:T(8,128)}, f32[4,1024]{1,0:T(4,128)}) custom-call(f32[5,1024,256]{2,1,0:T(8,128)S(1)} %get-tuple-element.10.dg_ref, f32[32,128]{1,0:T(8,128)S(1)} %get-tuple-element.11.pick_ref, s32[4,128,1024]{2,1,0:T(8,128)S(1)} %get-tuple-element.12.inv_ref, ...), custom_call_target="tpu_custom_call" | custom-call | tf_op jit(solution)/shard_map/weight_grads/pallas_call | solution.py:383

commit v7 on v6

--- a/solution.py
+++ b/solution.py
@@ -133,6 +133,8 @@
             src_ref=buf.at[other], dst_ref=buf.at[other], send_sem=s_sem,
             recv_sem=r_sem, device_id=peer, device_id_type=MESH).wait_recv()
 
+    pending = []
+
     def exchange(buf, me, n, peer, s_sem, r_sem, between=None):
         sends = [send(buf.at[me], buf.at[me], s_sem.at[i], r_sem.at[me], peer(i))
                  for i in range(n - 1, 0, -1)]
@@ -141,8 +143,7 @@
         for i in range(1, n):
             other = lax.rem(me + i, n)
             arrive(buf, other, s_sem.at[i], r_sem.at[other], peer(i))
-        for copy in sends:
-            copy.wait_send()
+        pending.extend(sends)
 
     def total(buf, n):
         acc = buf[0].astype(F32)
@@ -246,13 +247,14 @@
         rs_src[b] = rebuild(b).astype(BF16)
         if n > 0:
             sends.append(give(order[n - 1]))
-    rs_buf[q] = rebuild(q).astype(BF16)
+    piece = rebuild(q)
     sends.append(give(order[-1]))
     build_inverse()
-    for i in range(1, 8):
+    for i in (1, 7, 2, 6, 3, 5, 4):
         other = lax.rem(q + i, 8)
         arrive(rs_buf, other, rs_s.at[i], rs_r.at[other], qpeer(i))
-    hbuf[zh] = total(rs_buf, 8).astype(BF16)
+        piece = piece + rs_buf[other].astype(F32)
+    hbuf[zh] = piece.astype(BF16)
     copy = send(hbuf.at[zh], hbuf.at[zh], h_s, h_r.at[zh], hpeer)
     def spread(b, carry):
         for l in range(LAYERS):
@@ -260,10 +262,9 @@
         return carry
 
     lax.fori_loop(0, 8, spread, 0)
-    for other in sends:
-        other.wait_send()
+    pending.extend(sends)
     arrive(hbuf, 1 - zh, h_s, h_r.at[1 - zh], hpeer)
-    copy.wait_send()
+    pending.append(copy)
     rebuilt = total(hbuf, 2)
     for c in range(2):
         abuf[q, c] = (rebuilt[c] + dbias_v[pl.ds(c, 1), :] - goal[c]).astype(BF16)
@@ -290,8 +291,7 @@
         other = lax.rem(q + i, 8)
         arrive(abuf, other, ag_s.at[i], ag_r.at[other], qpeer(i))
         back(other)
-    for copy in sends:
-        copy.wait_send()
+    pending.extend(sends)
     lbuf[r] = pay_v[...].astype(BF16)
 
     def decoder_grads():
@@ -302,6 +302,8 @@
 
     exchange(lbuf, r, 16, lpeer, l_s, l_r, between=decoder_grads)
     pick_ref[...] = total(lbuf, 16).astype(BF16).astype(F32)
+    for copy in pending:
+        copy.wait_send()
 
 
 def main_call(x, enc, bias, dec, dbias, tgt, idx):

time: 42.9 us -> 43.3 us (level)
  Pallas kernels: 42.1 us -> 42.6 us
    pallas_call x1, Pallas kernels: 37.8 us -> 38.3 us  [main_call(): pl.pallas_call(main_kernel, out_shape=(jax.ShapeDtypeStruct((BLOCKS, WIDT...]
where the time goes in v7:
time: 43.3 us; the launch traced here: 43.2 us
  Pallas kernels  42.6 us (98%)
  between operations  0.64 us (1%)
    pallas_call x1, Pallas kernels, main_call(): pl.pallas_call(main_kernel, out_shape=(jax.ShapeDtypeStruct((BLOCKS, WIDT...  38.3 us
    pallas_call x1, Pallas kernels, grad_call(): pl.pallas_call(grad_kernel, out_shape=(jax.ShapeDtypeStruct((BLOCKS, WIDT...  4.32 us

profile of v7, /device:TPU:1, one launch (start us, length us, event | category | flops | bytes accessed | tf_op | source)
XLA Modules:
  0.0 43.2 jit_solution(12807613425048214608)
XLA Ops:
  0.6 38.3 %transcoder.1 = (f32[5,1024,256]{2,1,0:T(8,128)S(1)}, f32[32,128]{1,0:T(8,128)S(1)}, s32[4,128,1024]{2,1,0:T(8,128)S(1)}, bf16[4,128,128]{2,1,0:T(8,128)(2,1)S(1)}) custom-call(bf16[512,128]{1,0:T(8,128)(2,1)} %bitcast.7, bf16[4,128,1024]{2,1,0:T(8,128)(2,1)} %enc_hbm.1, f32[4,1024]{1,0:T(4,128)} %bias_hbm.1, bf16[5,1024,256]{2,1,0:T(8,128)(2,1)} %bitcast.6, ...), custom_call_target="tpu_custom_call" | custom-call | tf_op jit(solution)/shard_map/transcoder/pallas_call | solution.py:312
  38.9 4.3 %weight_grads.1 = (f32[5,1024,256]{2,1,0:T(8,128)}, f32[4,128,1024]{2,1,0:T(8,128)}, f32[4,1024]{1,0:T(4,128)}) custom-call(f32[5,1024,256]{2,1,0:T(8,128)S(1)} %get-tuple-element.10.dg_ref, f32[32,128]{1,0:T(8,128)S(1)} %get-tuple-element.11.pick_ref, s32[4,128,1024]{2,1,0:T(8,128)S(1)} %get-tuple-element.12.inv_ref, ...), custom_call_target="tpu_custom_call" | custom-call | tf_op jit(solution)/shard_map/weight_grads/pallas_call | solution.py:385
